TPU v7x, 256 devices: a whole 4x4x8 slice. The times are simulated.
256 devices in a mesh: gx: 8 (over z_hi, y), gz: 32 (over x, z_lo, core).
Axes of the slice: x: 4, y: 4, z: 8 (z_hi: 2, z_lo: 4; z = z_hi * 4 + z_lo), core: 2. Of those that a mesh axis runs over, the one named last changes fastest.
Arguments:
- state: float32 [5, 16, 128, 512], P(None, 'gx', 'gz'), may hold values from -21 to 21
- cotangent: float32 [5, 16, 128, 512], P(None, 'gx', 'gz'), may hold values from -6 to 6
- local_inverse: float32 [64, 16, 128, 512], P(None, 'gx', 'gz'), may hold values from -0.25 to 1.7
- wall_tags: int32 [2, 16, 128], P(None, 'gx', 'gz'), may hold values 0 or 1
- w_in: float32 [5, 256], replicated, may hold values from -2.5 to 2.5
- b_in: float32 [256], replicated, may hold values from -3 to 3
- w_mid: bfloat16 [256, 256], replicated, may hold values from -0.375 to 0.375
- b_mid: float32 [256], replicated, may hold values from -3 to 3
- w_out: bfloat16 [256, 5], replicated, may hold values from -1.5 to 1.5
Outputs:
- grad_state: float32 [5, 16, 128, 512], P(None, 'gx', 'gz')
- grad_w_in: float32 [5, 256], replicated
- grad_b_in: float32 [256], replicated
- grad_w_mid: float32 [256, 256], replicated
- grad_b_mid: float32 [256], replicated
- grad_w_out: float32 [256, 5], replicated
All inputs are finite; a program needn't handle non-finite values. No bound on the sum of `wall_tags` on one device may be relied on, other than what follows from the above.
Results may differ from a plain program's by a relative error of at most 0.0085.
Values sent between devices are 32-bit elements; how exact they have to be, the bound alone decides.
No kernel may reach another device: no remote copies, remote signals or barrier semaphores. Data moves between devices by JAX's collectives and lax.ppermute only.
A program may use at most 64 MiB of HBM per device.

v0:
```python
import math

import jax
import jax.numpy as jnp
from jax import lax
from jax.sharding import PartitionSpec as P

KAPPA = 0.5
DT_STEP = 0.5
EPS = 1e-06
precise = lax.Precision.HIGHEST


def extended(cells, sides, width):
    for axis, dim in sides:
        count = lax.axis_size(axis)
        head = lax.slice_in_dim(cells, 0, width, axis=dim)
        tail = lax.slice_in_dim(cells, cells.shape[dim] - width, cells.shape[dim], axis=dim)
        cells = jnp.concatenate(
            [
                lax.ppermute(tail, axis, [(i, (i + 1) % count) for i in range(count)]),
                cells,
                lax.ppermute(head, axis, [((i + 1) % count, i) for i in range(count)]),
            ],
            axis=dim,
        )
    return cells


def silu_slope(pre_act):
    sigmoid_value = jax.nn.sigmoid(pre_act)
    return sigmoid_value * (1.0 + pre_act * (1.0 - sigmoid_value))


def inner_rows(first_op, second_op, precision=None):
    return lax.dot_general(
        first_op,
        second_op,
        (((1,), (1,)), ((), ())),
        precision=precision,
        preferred_element_type=jnp.float32,
    )


def inner_first(first_op, second_op, precision=None):
    return lax.dot_general(
        first_op,
        second_op,
        (((0,), (0,)), ((), ())),
        precision=precision,
        preferred_element_type=jnp.float32,
    )


def face_terms(blocks_view, lower_nb, upper_nb, face_axis):
    lower_term = 0.5 * (lower_nb - jnp.take(blocks_view, 0, axis=face_axis))
    upper_term = 0.5 * (upper_nb - jnp.take(blocks_view, 3, axis=face_axis))
    zero_face = jnp.zeros_like(lower_term)
    return jnp.stack([lower_term, zero_face, zero_face, upper_term], axis=face_axis)


def coupling(blocks_view, lower_x, upper_x, lower_z, upper_z, wall_tags):
    bottom = (1.0 - 2.0 * wall_tags[0].astype(jnp.float32))[None, :, :, None, None, None]
    top_side = (1.0 - 2.0 * wall_tags[1].astype(jnp.float32))[None, :, :, None, None, None]
    lower_y = jnp.concatenate(
        [bottom * blocks_view[:, :, :, :1, :, 0, :], blocks_view[:, :, :, :-1, :, 3, :]], axis=3
    )
    upper_y = jnp.concatenate(
        [blocks_view[:, :, :, 1:, :, 0, :], top_side * blocks_view[:, :, :, -1:, :, 3, :]], axis=3
    )
    return (
        face_terms(blocks_view, lower_x, upper_x, 4)
        + face_terms(blocks_view, lower_y, upper_y, 5)
        + face_terms(blocks_view, lower_z, upper_z, 6)
    )


def per_device(state, cotangent, local_inverse, wall_tags, w_in, b_in, w_mid, b_mid, w_out):
    channels, x_elems, z_elems, line_nodes = state.shape
    y_elems = line_nodes // 64
    node_rows = x_elems * z_elems * line_nodes
    entry_count = channels * node_rows * lax.axis_size("gx") * lax.axis_size("gz")
    sum_squares = lax.psum(jnp.sum(state * state), ("gx", "gz"))
    inv_norm = lax.rsqrt(sum_squares / entry_count + EPS)
    adjoint = jnp.einsum(
        "nikjm,cikjn->cikjm",
        local_inverse.reshape(64, x_elems, z_elems, y_elems, 64),
        cotangent.reshape(channels, x_elems, z_elems, y_elems, 64),
        precision=precise,
    )
    adjoint_flat = adjoint.reshape(channels, x_elems, z_elems, line_nodes)
    blocks_view = adjoint.reshape(channels, x_elems, z_elems, y_elems, 4, 4, 4)
    padded = extended(adjoint_flat, (("gx", 1), ("gz", 2)), 1)
    padded_view = padded.reshape(channels, x_elems + 2, z_elems + 2, y_elems, 4, 4, 4)
    lower_x = padded_view[:, :-2, 1:-1, :, 3]
    upper_x = padded_view[:, 2:, 1:-1, :, 0]
    lower_z = padded_view[:, 1:-1, :-2, :, :, :, 3]
    upper_z = padded_view[:, 1:-1, 2:, :, :, :, 0]
    coupled = coupling(blocks_view, lower_x, upper_x, lower_z, upper_z, wall_tags).reshape(
        channels, x_elems, z_elems, line_nodes
    )
    state_rows = state.reshape(channels, node_rows)
    scaled_rows = inv_norm * state_rows
    pre_first = inner_first(w_in, scaled_rows, precise) + b_in[:, None]
    hidden_one = jax.nn.silu(pre_first).astype(jnp.bfloat16)
    pre_second = inner_first(w_mid, hidden_one) + b_mid[:, None]
    hidden_two = jax.nn.silu(pre_second).astype(jnp.bfloat16)
    out_grad = (DT_STEP * adjoint_flat.reshape(channels, node_rows)).astype(jnp.bfloat16)
    grad_out = inner_rows(hidden_two, out_grad)
    back_two = jnp.dot(w_out, out_grad, preferred_element_type=jnp.float32)
    delta_two = (back_two * silu_slope(pre_second)).astype(jnp.bfloat16)
    grad_mid = inner_rows(hidden_one, delta_two)
    grad_bmid = jnp.sum(delta_two, axis=1, dtype=jnp.float32)
    back_one = jnp.dot(w_mid, delta_two, preferred_element_type=jnp.float32)
    delta_one = back_one * silu_slope(pre_first)
    grad_in = inner_rows(scaled_rows, delta_one, precise)
    grad_bin = jnp.sum(delta_one, axis=1)
    back_input = jnp.dot(w_in, delta_one, precision=precise, preferred_element_type=jnp.float32)
    grad_state = (
        adjoint_flat
        + KAPPA * coupled
        + inv_norm * back_input.reshape(channels, x_elems, z_elems, line_nodes)
    )
    summed = lax.psum((grad_in, grad_bin, grad_mid, grad_bmid, grad_out), ("gx", "gz"))
    factor = 4.0 / math.sqrt(entry_count // channels)
    return (
        grad_state,
        summed[0] * factor,
        summed[1] * factor,
        summed[2] * factor,
        summed[3] * factor,
        summed[4] * factor,
    )


def solution(mesh):
    placed = (
        P(None, "gx", "gz", None),
        P(None, "gx", "gz", None),
        P(None, "gx", "gz", None),
        P(None, "gx", "gz"),
        P(),
        P(),
        P(),
        P(),
        P(),
    )
    return jax.shard_map(
        per_device,
        mesh=mesh,
        in_specs=placed,
        out_specs=(P(None, "gx", "gz", None), P(), P(), P(), P(), P()),
        check_vma=False,
    )
```

profile of v0, /device:TPU:2, one launch (start us, length us, event | category | flops | bytes accessed | tf_op | source)
XLA Modules:
  0.0 372.4 jit_solution(2439335443152429665)
XLA Ops:
  7.3 1.9 reshape.105
  9.1 1.0 reshape.104
  10.1 2.9 fusion.8
  13.1 0.1 reshape.106
  13.2 0.6 fusion.34
  13.9 1.6 collective-permute-start
  15.4 0.6 multiply_reduce_fusion
  16.1 8.1 %collective-permute-start.1 = (f32[5,1,4,512]{3,2,1,0:T(4,128)}, f32[5,1,4,512]{3,2,1,0:T(4,128)}, u32[]{:S(2)}, u32[]{:S(2)}) collective-permute-start(f32[5,1,4,512]{3,2,1,0:T(4,128)} %get-tuple-element.100), channel_id=1, source_target_pairs={{32,0},{64,32},{96,64},{128,96},{160,128},{192,160},{224,192},{0,2... | collective-permute-start | bytes 122888 | tf_op jit(solution)/shard_map/ppermute | solution.py:23
  24.1 75.8 %psum.42 = f32[]{:T(128)} all-reduce(f32[]{:T(128)} %multiply_reduce_fusion), channel_id=1, replica_groups=mesh['gx'=8,'gz'=32] {'gx','gz'}, use_global_device_ids=true, to_apply=%region_1.8 | all-reduce | flops 1 | bytes 8 | tf_op jit(solution)/shard_map/psum | solution.py:83
  100.8 0.1 convert_element_type.37
  100.9 5.8 %multiply_convert_fusion.1 = (bf16[256,4096]{0,1:T(8,128)(2,1)S(1)}, f32[256,4096]{0,1:T(8,128)}) fusion(f32[256]{0:T(256)S(1)} %copy-done.11, f32[5,4096]{1,0:T(8,128)S(1)} %mul.176, f32[5,256]{1,0:T(8,128)S(1)} %copy-done.6), kind=kOutput, calls=%fused_computation.14 | convolution fusion | flops 69206016 | bytes 6379520 | tf_op jit(solution)/shard_map/dot_general | solution.py:46
  106.8 0.7 fusion.1
  107.5 1.8 convert_reduce_fusion
  109.3 0.1 copy-done.3
  109.5 1.4 copy-done.12
  110.9 1.4 fusion.37
  112.3 0.4 copy.149
  112.8 0.2 fusion.32
  113.0 0.2 slice_bitcast_fusion.3
  113.3 1.5 fusion.31
  114.8 4.6 %fusion.35 = (f32[256]{0:T(256)S(1)}, f32[256,4096]{0,1:T(8,128)S(1)}) fusion(f32[256,4096]{0,1:T(8,128)} %get-tuple-element.105, bf16[256,4096]{0,1:T(8,128)(2,1)} %copy-done.12, bf16[256,256]{1,0:T(8,128)(2,1)S(1)} %copy-done), kind=kOutput, calls=%fused_computation.72 | convolution fusion | flops 546307840 | bytes 10617856 | tf_op jit(solution)/shard_map/dot_general | solution.py:114
  119.4 3.6 fusion.5
  123.0 1.7 fusion.36
  124.7 1.2 fusion.10
  125.9 1.1 copy.155
  127.0 1.1 copy.156
  128.1 0.9 copy.160
  129.0 1.1 copy.161
  130.1 74.0 %all-reduce = (f32[5,256]{1,0:T(8,128)S(1)}, f32[256]{0:T(256)S(1)}, f32[256]{0:T(256)S(1)}, f32[256,5]{0,1:T(8,128)S(1)}) all-reduce(f32[5,256]{1,0:T(8,128)S(1)} %fusion.36, f32[256]{0:T(256)S(1)} %get-tuple-element.106, f32[256]{0:T(256)S(1)} %get-tuple-element.108, ...), channel_id=1, replica_groups=mesh['gx'=8,'gz'=32] {'gx','gz'}, use_global_device_ids=true, to_apply=%region_2.9 | all-reduce | flops 3072 | bytes 24576 | tf_op jit(solution)/shard_map/psum | solution.py:124
  204.1 0.6 broadcast_multiply_fusion.4
  204.7 1.0 broadcast_multiply_fusion
  205.8 0.6 broadcast_multiply_fusion.5
  206.4 0.8 constant_dynamic-update-slice_fusion.2
  207.2 0.8 constant_dynamic-update-slice_fusion
  208.0 0.1 fusion.33
  208.0 0.1 collective-permute-start.2
  208.1 4.4 %collective-permute-start.3 = (f32[5,4,1,512]{3,2,1,0:T(1,128)S(1)}, f32[5,4,1,512]{3,2,1,0:T(1,128)S(1)}, u32[]{:S(2)}, u32[]{:S(2)}) collective-permute-start(f32[5,4,1,512]{3,2,1,0:T(1,128)S(1)} %get-tuple-element.99), channel_id=1, source_target_pairs={{1,0},{2,1},{3,2},{4,3},{5,4},{6,5},{7,6},{8,7},{9,8},{10,9},{11,1... | collective-permute-start | bytes 122888 | tf_op jit(solution)/shard_map/ppermute | solution.py:23
  212.5 0.6 broadcast_multiply_fusion.6
  213.1 0.7 mul.186
  213.8 0.1 pad.23.clone
  213.9 0.5 collective-permute-done.2
  214.4 0.1 pad_maximum_fusion
  214.5 0.2 copy.147
  214.7 11.8 %reshape.107 = f32[5,4,6,8,4,4,4]{6,5,4,3,1,2,0:T(4,128)} reshape(f32[5,4,6,512]{3,1,2,0:T(4,128)S(1)} %copy.147) | data formatting | bytes 491520 | tf_op jit(solution)/shard_map/reshape | solution.py:94
  226.5 1.4 fusion.30
  227.9 7.0 %fusion.29 = (f32[5,2,4,8,4,4,1]{6,5,4,3,1,2,0:T(4,128)}, f32[5,2,4,8,4,4,1]{6,5,4,3,1,2,0:T(4,128)}) fusion(f32[5,4,6,8,4,4,4]{6,5,4,3,1,2,0:T(4,128)} %reshape.107), kind=kLoop, calls=%fused_computation.66 | loop fusion | bytes 81920 | tf_op jit(solution)/shard_map/slice | solution.py:97
  234.9 1.7 copy.171
  236.7 1.0 copy.173
  237.7 2.7 fusion.16
  240.4 1.0 copy.153
  241.4 1.9 copy.154
  243.2 2.9 copy.163
  246.1 2.7 copy.164
  248.8 5.8 %copy.165 = f32[5,2,4,8,4,4,1]{3,5,6,4,2,1,0:T(4,128)} copy(f32[5,2,4,8,4,4,1]{6,5,4,3,1,2,0:T(4,128)} %get-tuple-element.84) | data formatting | bytes 40960 | tf_op jit(solution)/shard_map/slice | solution.py:97
  254.7 1.9 fusion.26
  256.6 5.8 %copy.168 = f32[5,2,4,8,4,4,1]{6,5,4,3,2,1,0:T(4,128)} copy(f32[5,2,4,8,4,4,1]{3,5,4,2,1,0,6:T(4,128)} %fusion.26) | data formatting | bytes 40960 | tf_op jit(solution)/shard_map/stack | solution.py:59
  262.4 4.7 %copy.167 = f32[5,2,4,8,4,4,1]{3,5,6,4,2,1,0:T(4,128)} copy(f32[5,2,4,8,4,4,1]{6,5,4,3,1,2,0:T(4,128)S(1)} %copy-done.1) | data formatting | bytes 40960 | tf_op jit(solution)/shard_map/slice | solution.py:98
  267.1 2.1 fusion.24
  269.2 5.8 %copy.169 = f32[5,2,4,8,4,4,1]{6,5,4,3,2,1,0:T(4,128)} copy(f32[5,2,4,8,4,4,1]{3,5,4,2,1,0,6:T(4,128)} %fusion.24) | data formatting | bytes 40960 | tf_op jit(solution)/shard_map/stack | solution.py:59
  275.0 6.3 %fusion.7 = f32[5,2,4,8,4,4,4]{6,5,4,3,2,1,0:T(4,128)} fusion(f32[5,2,4,8,1,4,4]{6,5,4,3,2,1,0:T(4,128)} %copy.154, f32[5,2,4,8,1,4,4]{6,5,4,3,2,1,0:T(4,128)S(1)} %copy.153, f32[5,2,4,8,4,1,4]{6,5,4,3,2,1,0:T(1,128)} %copy.164, f32[5,2,4,8,4,1,4]{6,5,4,3,2,1,0:T(1,128)} %copy.163, f32[5,2,4,8,4,4,1]{6,5,4,3,2,1,0:T(4,128)} %copy.169, ...), kind=kLoop, calls=%fused_computation.18 | loop fusion | flops 184320 | bytes 204816 | tf_op jit(solution)/shard_map/mul | solution.py:121
  281.3 4.1 %mul.169 = f32[5,2,4,512]{3,2,1,0:T(4,128)S(1)} reshape(f32[5,2,4,8,4,4,4]{6,5,4,3,2,1,0:T(4,128)} %fusion.7) | data formatting | bytes 163840 | tf_op jit(solution)/shard_map/mul | solution.py:121
  285.5 1.5 add_add_fusion
  287.0 76.5 %all-reduce.3.cloned.1.call-done = f32[256,256]{1,0:T(8,128)} async-done(((f32[256,256]{1,0:T(8,128)}), f32[256,256]{1,0:T(8,128)}) %all-reduce.3.cloned.1.call-update) | async-done | bytes 262160 | tf_op jit(solution)/shard_map/psum | solution.py:124
  363.5 1.7 broadcast_multiply_fusion.2
  (35 shorter events, 0.3 us)
Async XLA Ops:
  7.2 99.6 %copy-start = (bf16[256,256]{1,0:T(8,128)(2,1)S(1)}, bf16[256,256]{1,0:T(8,128)(2,1)}, u32[]{:S(2)}) copy-start(bf16[256,256]{1,0:T(8,128)(2,1)} %param.27) | copy-start | bytes 393220
  7.2 8.3 %copy-start.5 = (f32[5,2,4,512]{3,2,1,0:T(4,128)S(1)}, f32[5,2,4,512]{3,2,1,0:T(4,128)}, u32[]{:S(2)}) copy-start(f32[5,2,4,512]{3,2,1,0:T(4,128)} %param.21) | copy-start | bytes 245764
  7.2 93.7 %copy-start.6 = (f32[5,256]{1,0:T(8,128)S(1)}, f32[5,256]{1,0:T(8,128)}, u32[]{:S(2)}) copy-start(f32[5,256]{1,0:T(8,128)} %param.25) | copy-start | bytes 15364
  7.2 93.7 %copy-start.11 = (f32[256]{0:T(256)S(1)}, f32[256]{0:T(256)}, u32[]{:S(2)}) copy-start(f32[256]{0:T(256)} %param.26) | copy-start | bytes 3076
  7.2 356.3 %all-reduce.3.cloned.1.call-start = ((), (), s32[]{:S(2)}) async-start(), calls=%async_computation | async-start | bytes 524288 | tf_op jit(solution)/shard_map/psum | solution.py:124
  13.9 192.5 %collective-permute-start = (f32[5,1,4,512]{3,2,1,0:T(4,128)}, f32[5,1,4,512]{3,2,1,0:T(4,128)}, u32[]{:S(2)}, u32[]{:S(2)}) collective-permute-start(f32[5,1,4,512]{3,2,1,0:T(4,128)} %get-tuple-element.101), channel_id=1, source_target_pairs={{0,32},{32,64},{64,96},{96,128},{128,160},{160,192},{192,224},{224... | collective-permute-start | bytes 122888 | tf_op jit(solution)/shard_map/ppermute | solution.py:21
  16.1 191.1 %collective-permute-start.1 = (f32[5,1,4,512]{3,2,1,0:T(4,128)}, f32[5,1,4,512]{3,2,1,0:T(4,128)}, u32[]{:S(2)}, u32[]{:S(2)}) collective-permute-start(f32[5,1,4,512]{3,2,1,0:T(4,128)} %get-tuple-element.100), channel_id=1, source_target_pairs={{32,0},{64,32},{96,64},{128,96},{160,128},{192,160},{224,192},{0,2... | collective-permute-start | bytes 122888 | tf_op jit(solution)/shard_map/ppermute | solution.py:23
  100.9 5.9 %copy-start.8 = (f32[256]{0:T(256)S(1)}, f32[256]{0:T(256)}, u32[]{:S(2)}) copy-start(f32[256]{0:T(256)} %param.28) | copy-start | bytes 3076
  106.8 0.7 copy-start.10
  107.5 2.0 copy-start.3
  109.5 1.4 copy-start.12
  114.8 4.6 %copy-start.7 = (f32[5,256]{1,0:T(8,128)S(1)}, f32[5,256]{1,0:T(8,128)}, u32[]{:S(2)}) copy-start(f32[5,256]{1,0:T(8,128)} %param.25) | copy-start | bytes 15364
  119.4 5.4 %copy-start.4 = (f32[256,4096]{0,1:T(8,128)S(1)}, f32[256,4096]{0,1:T(8,128)}, u32[]{:S(2)}) copy-start(f32[256,4096]{0,1:T(8,128)} %copy-done.3) | copy-start | bytes 12582916
  124.7 5.4 %copy-start.9 = (s32[2,2,4]{2,1,0:T(2,128)S(1)}, s32[2,2,4]{2,1,0:T(2,128)}, u32[]{:S(2)}) copy-start(s32[2,2,4]{2,1,0:T(2,128)} %param.24) | copy-start | bytes 196
  208.0 6.4 %collective-permute-start.2 = (f32[5,4,1,512]{3,2,1,0:T(1,128)S(1)}, f32[5,4,1,512]{3,2,1,0:T(1,128)S(1)}, u32[]{:S(2)}, u32[]{:S(2)}) collective-permute-start(f32[5,4,1,512]{3,2,1,0:T(1,128)S(1)} %get-tuple-element.98), channel_id=1, source_target_pairs={{0,1},{1,2},{2,3},{3,4},{4,5},{5,6},{6,7},{7,8},{8,9},{9,10},{10,1... | collective-permute-start | bytes 122888 | tf_op jit(solution)/shard_map/ppermute | solution.py:21
  208.1 6.3 %collective-permute-start.3 = (f32[5,4,1,512]{3,2,1,0:T(1,128)S(1)}, f32[5,4,1,512]{3,2,1,0:T(1,128)S(1)}, u32[]{:S(2)}, u32[]{:S(2)}) collective-permute-start(f32[5,4,1,512]{3,2,1,0:T(1,128)S(1)} %get-tuple-element.99), channel_id=1, source_target_pairs={{1,0},{2,1},{3,2},{4,3},{5,4},{6,5},{7,6},{8,7},{9,8},{10,9},{11,1... | collective-permute-start | bytes 122888 | tf_op jit(solution)/shard_map/ppermute | solution.py:23
  243.2 19.2 %copy-start.1 = (f32[5,2,4,8,4,4,1]{6,5,4,3,1,2,0:T(4,128)S(1)}, f32[5,2,4,8,4,4,1]{6,5,4,3,1,2,0:T(4,128)}, u32[]{:S(2)}) copy-start(f32[5,2,4,8,4,4,1]{6,5,4,3,1,2,0:T(4,128)} %get-tuple-element.85) | copy-start | bytes 61444
  267.1 7.9 %copy-start.2 = (f32[5,2,4,8,4,4,1]{6,5,4,3,2,1,0:T(4,128)S(1)}, f32[5,2,4,8,4,4,1]{6,5,4,3,2,1,0:T(4,128)}, u32[]{:S(2)}) copy-start(f32[5,2,4,8,4,4,1]{6,5,4,3,2,1,0:T(4,128)} %copy.168) | copy-start | bytes 61444
Sparse Core Ops, SparseCore 0:
  112.5 250.9 all-reduce.2
where the time goes:
time: 379 us; the launch traced here: 372 us
  blocking collectives  150 us (40%)
  waiting for transfers between devices  77 us (20%)
  local copies, waits for them, and re-layouts  72.3 us (19%)
  matrix products  23.9 us (6%)
  other arithmetic  19.8 us (5%)
  between operations  15.5 us (4%)
  starting transfers between devices  14.2 us (4%)
    psum x1, waiting for transfers between devices, per_device(): lax.psum((grad_in, grad_bin, grad_mid, grad_bmid, grad_out), ('gx', 'gz'))  76.5 us
    psum x1, blocking collectives, per_device(): sum_squares = lax.psum(jnp.sum(state * state), ('gx', 'gz'))  75.8 us
    psum x1, blocking collectives, per_device(): lax.psum((grad_in, grad_bin, grad_mid, grad_bmid, grad_out), ('gx', 'gz'))  74 us
    another operation x8, local copies, waits for them, and re-layouts, face_terms(): jnp.stack([lower_term, zero_face, zero_face, upper_term], axis=face_axis)  20.2 us
    slice x2, local copies, waits for them, and re-layouts, per_device(): lower_z = padded_view[:, 1:-1, :-2, :, :, :, 3]  12.8 us
    ppermute x2, starting transfers between devices, extended(): lax.ppermute(head, axis, [((i + 1) % count, i) for i in range(count)])  12.5 us
    reshape x1, local copies, waits for them, and re-layouts, per_device(): padded.reshape(channels, x_elems + 2, z_elems + 2, y_elems, 4, 4, 4)  11.8 us
  transfers between devices with their start and end apart: 5, of which 2 were waited for; matrix products, arithmetic and copies ran while one was open for 28% of the time, Pallas kernels for 0%

commit v1 on v0

--- a/solution.py
+++ b/solution.py
@@ -2,29 +2,19 @@
 
 import jax
 import jax.numpy as jnp
+import numpy as np
 from jax import lax
-from jax.sharding import PartitionSpec as P
+from jax.sharding import Mesh, PartitionSpec as P
 
 KAPPA = 0.5
 DT_STEP = 0.5
 EPS = 1e-06
 precise = lax.Precision.HIGHEST
 
-
-def extended(cells, sides, width):
-    for axis, dim in sides:
-        count = lax.axis_size(axis)
-        head = lax.slice_in_dim(cells, 0, width, axis=dim)
-        tail = lax.slice_in_dim(cells, cells.shape[dim] - width, cells.shape[dim], axis=dim)
-        cells = jnp.concatenate(
-            [
-                lax.ppermute(tail, axis, [(i, (i + 1) % count) for i in range(count)]),
-                cells,
-                lax.ppermute(head, axis, [((i + 1) % count, i) for i in range(count)]),
-            ],
-            axis=dim,
-        )
-    return cells
+AXES = ("zhi", "y", "x", "zlo", "core")
+GX = ("zhi", "y")
+GZ = ("x", "zlo", "core")
+CHIPS = ("zhi", "y", "x", "zlo")
 
 
 def silu_slope(pre_act):
@@ -75,12 +65,43 @@
     )
 
 
+def ring(count, step):
+    return [(i, (i + step) % count) for i in range(count)]
+
+
+def all_devices_sum(value, count):
+    spread = jnp.broadcast_to(value, (count, 1, 128))
+    return jnp.sum(lax.all_to_all(spread, AXES, 0, 0, tiled=True)[:, 0, 0])
+
+
+def reduce_everywhere(packed, chips, factor):
+    rows, width = packed.shape
+    halves = packed.reshape(2, rows // 2, width)
+    core = lax.axis_index("core")
+    swap = [(0, 1), (1, 0)]
+    mine = lax.dynamic_index_in_dim(halves, core, 0, False)
+    other = lax.dynamic_index_in_dim(halves, 1 - core, 0, False)
+    mine = mine + lax.ppermute(other, "core", swap)
+    scattered = lax.all_to_all(mine.reshape(chips, -1, width), CHIPS, 0, 0, tiled=True)
+    chunk = factor * jnp.sum(scattered, axis=0)
+    chunk = lax.optimization_barrier(chunk)
+    gathered = lax.all_to_all(
+        jnp.broadcast_to(chunk[None], (chips,) + chunk.shape), CHIPS, 0, 0, tiled=True
+    )
+    gathered = lax.optimization_barrier(gathered)
+    partner = lax.ppermute(gathered, "core", swap)
+    first = jnp.where(core == 0, gathered, partner)
+    second = jnp.where(core == 0, partner, gathered)
+    return jnp.concatenate([first, second], axis=0).reshape(rows, width)
+
+
 def per_device(state, cotangent, local_inverse, wall_tags, w_in, b_in, w_mid, b_mid, w_out):
     channels, x_elems, z_elems, line_nodes = state.shape
     y_elems = line_nodes // 64
     node_rows = x_elems * z_elems * line_nodes
-    entry_count = channels * node_rows * lax.axis_size("gx") * lax.axis_size("gz")
-    sum_squares = lax.psum(jnp.sum(state * state), ("gx", "gz"))
+    gx, gz = lax.axis_size(GX), lax.axis_size(GZ)
+    entry_count = channels * node_rows * gx * gz
+    sum_squares = all_devices_sum(jnp.sum(state * state), gx * gz)
     inv_norm = lax.rsqrt(sum_squares / entry_count + EPS)
     adjoint = jnp.einsum(
         "nikjm,cikjn->cikjm",
@@ -90,12 +111,14 @@
     )
     adjoint_flat = adjoint.reshape(channels, x_elems, z_elems, line_nodes)
     blocks_view = adjoint.reshape(channels, x_elems, z_elems, y_elems, 4, 4, 4)
-    padded = extended(adjoint_flat, (("gx", 1), ("gz", 2)), 1)
-    padded_view = padded.reshape(channels, x_elems + 2, z_elems + 2, y_elems, 4, 4, 4)
-    lower_x = padded_view[:, :-2, 1:-1, :, 3]
-    upper_x = padded_view[:, 2:, 1:-1, :, 0]
-    lower_z = padded_view[:, 1:-1, :-2, :, :, :, 3]
-    upper_z = padded_view[:, 1:-1, 2:, :, :, :, 0]
+    from_left = lax.ppermute(blocks_view[:, -1:, :, :, 3], GX, ring(gx, 1))
+    from_right = lax.ppermute(blocks_view[:, :1, :, :, 0], GX, ring(gx, -1))
+    from_front = lax.ppermute(blocks_view[:, :, -1:, :, :, :, 3], GZ, ring(gz, 1))
+    from_back = lax.ppermute(blocks_view[:, :, :1, :, :, :, 0], GZ, ring(gz, -1))
+    lower_x = jnp.concatenate([from_left, blocks_view[:, :-1, :, :, 3]], axis=1)
+    upper_x = jnp.concatenate([blocks_view[:, 1:, :, :, 0], from_right], axis=1)
+    lower_z = jnp.concatenate([from_front, blocks_view[:, :, :-1, :, :, :, 3]], axis=2)
+    upper_z = jnp.concatenate([blocks_view[:, :, 1:, :, :, :, 0], from_back], axis=2)
     coupled = coupling(blocks_view, lower_x, upper_x, lower_z, upper_z, wall_tags).reshape(
         channels, x_elems, z_elems, line_nodes
     )
@@ -113,7 +136,7 @@
     grad_bmid = jnp.sum(delta_two, axis=1, dtype=jnp.float32)
     back_one = jnp.dot(w_mid, delta_two, preferred_element_type=jnp.float32)
     delta_one = back_one * silu_slope(pre_first)
-    grad_in = inner_rows(scaled_rows, delta_one, precise)
+    grad_in = inner_rows(delta_one, scaled_rows, precise)
     grad_bin = jnp.sum(delta_one, axis=1)
     back_input = jnp.dot(w_in, delta_one, precision=precise, preferred_element_type=jnp.float32)
     grad_state = (
@@ -121,34 +144,32 @@
         + KAPPA * coupled
         + inv_norm * back_input.reshape(channels, x_elems, z_elems, line_nodes)
     )
-    summed = lax.psum((grad_in, grad_bin, grad_mid, grad_bmid, grad_out), ("gx", "gz"))
     factor = 4.0 / math.sqrt(entry_count // channels)
+    hidden = w_mid.shape[0]
+    pad = jnp.zeros((hidden, 384 - hidden - 2 * channels - 2), jnp.float32)
+    packed = jnp.concatenate(
+        [grad_mid, grad_in, grad_out, grad_bin[:, None], grad_bmid[:, None], pad], axis=1
+    )
+    summed = reduce_everywhere(packed, gx * gz // 2, factor)
+    h, c = hidden, channels
     return (
         grad_state,
-        summed[0] * factor,
-        summed[1] * factor,
-        summed[2] * factor,
-        summed[3] * factor,
-        summed[4] * factor,
+        summed[:, h : h + c].T,
+        summed[:, h + 2 * c],
+        summed[:, :h],
+        summed[:, h + 2 * c + 1],
+        summed[:, h + c : h + 2 * c],
     )
 
 
 def solution(mesh):
-    placed = (
-        P(None, "gx", "gz", None),
-        P(None, "gx", "gz", None),
-        P(None, "gx", "gz", None),
-        P(None, "gx", "gz"),
-        P(),
-        P(),
-        P(),
-        P(),
-        P(),
-    )
+    fine = Mesh(mesh.devices.reshape(2, 4, 4, 4, 2), AXES)
+    block = P(None, GX, GZ, None)
+    placed = (block, block, block, P(None, GX, GZ)) + (P(),) * 5
     return jax.shard_map(
         per_device,
-        mesh=mesh,
+        mesh=fine,
         in_specs=placed,
-        out_specs=(P(None, "gx", "gz", None), P(), P(), P(), P(), P()),
+        out_specs=(block, P(), P(), P(), P(), P()),
         check_vma=False,
     )

time: 379 us -> 182 us (0.48)
  the two profiles are of different devices: /device:TPU:2 before, /device:TPU:1 now
where the time goes in v1:
time: 182 us; the launch traced here: 180 us
  starting transfers between devices  66.6 us (37%)
  local copies, waits for them, and re-layouts  57 us (31%)
  matrix products  36.2 us (20%)
  other arithmetic  17.5 us (10%)
  between operations  2.15 us (1%)
    ppermute x1, starting transfers between devices, per_device(): from_right = lax.ppermute(blocks_view[:, :1, :, :, 0], GX, ring(gx, -1))  18.6 us
    all_to_all x1, starting transfers between devices, all_devices_sum(): return jnp.sum(lax.all_to_all(spread, AXES, 0, 0, tiled=True)[:, 0, 0])  16.6 us
    another operation x8, local copies, waits for them, and re-layouts, face_terms(): jnp.stack([lower_term, zero_face, zero_face, upper_term], axis=face_axis)  16.1 us
    all_to_all x1, starting transfers between devices, reduce_everywhere(): lax.all_to_all(jnp.broadcast_to(chunk[None], (chips,) + chunk.shape), CHI...  13.6 us
    all_to_all x1, starting transfers between devices, reduce_everywhere(): lax.all_to_all(mine.reshape(chips, -1, width), CHIPS, 0, 0, tiled=True)  9.71 us
    dot_general x2, matrix products, inner_first(): lax.dot_general(first_op, second_op, (((0,), (0,)), ((), ())), precision=...  9.45 us
    dot_general x3, matrix products, inner_rows(): lax.dot_general(first_op, second_op, (((1,), (1,)), ((), ())), precision=...  8.88 us
    dot_general x2, local copies, waits for them, and re-layouts, inner_rows(): lax.dot_general(first_op, second_op, (((1,), (1,)), ((), ())), precision=...  8.56 us
  transfers between devices with their start and end apart: 9, of which 1 were waited for; matrix products, arithmetic and copies ran while one was open for 56% of the time, Pallas kernels for 0%

profile of v1, /device:TPU:1, one launch (start us, length us, event | category | flops | bytes accessed | tf_op | source)
XLA Modules:
  0.0 180.0 jit_solution(6869379457447066230)
XLA Ops:
  0.6 1.6 multiply_reduce_fusion
  2.2 1.4 broadcast_in_dim.26
  3.6 16.6 %all-to-all-start = ((f32[256,1,128]{2,1,0:T(1,128)}), f32[256,1,128]{2,1,0:T(1,128)}, u32[]{:S(2)}, u32[]{:S(2)}) async-start(f32[256,1,128]{2,1,0:T(1,128)} %broadcast_in_dim.26), calls=%async_computation | async-start | bytes 262144 | tf_op jit(solution)/shard_map/all_to_all | solution.py:74
  20.2 1.0 reshape.134
  21.2 1.8 %reshape.135 = f32[64,2,4,8,64]{4,3,2,1,0:T(8,128)S(1)} reshape(f32[64,2,4,512]{3,2,1,0:T(4,128)} %param.23) | data formatting | bytes 2097152 | tf_op jit(solution)/shard_map/reshape | solution.py:108
  23.1 3.7 %fusion.8 = f32[2,4,8,5,64]{4,3,2,1,0:T(8,128)} fusion(f32[64,2,4,8,64]{4,3,2,1,0:T(8,128)S(1)} %reshape.135, f32[5,2,4,8,64]{4,3,2,1,0:T(8,128)S(1)} %reshape.134), kind=kOutput, calls=%fused_computation.19 | convolution fusion | flops 15728640 | bytes 1212416 | tf_op jit(solution)/shard_map/nikjm,cikjn->cikjm/dot_general | solution.py:106
  26.7 1.4 copy.288
  28.2 0.8 fusion.27
  29.0 2.2 %collective-permute-start.3 = (f32[5,2,1,8,4,4]{3,5,4,1,0,2:T(4,128)}, f32[5,2,1,8,4,4]{3,5,4,1,0,2:T(4,128)}, u32[]{:S(2)}, u32[]{:S(2)}) collective-permute-start(f32[5,2,1,8,4,4]{3,5,4,1,0,2:T(4,128)} %bitcast.26), channel_id=1, source_target_pairs={{0,31},{1,0},{2,1},{3,2},{4,3},{5,4},{6,5},{7,6},{8,7},{9,8},{10,9... | collective-permute-start | bytes 15368 | tf_op jit(solution)/shard_map/ppermute | solution.py:117
  31.2 0.9 slice_bitcast_fusion.9
  32.1 0.9 collective-permute-start
  33.0 18.6 %collective-permute-start.1 = (f32[5,1,4,8,4,4]{3,5,4,2,1,0:T(4,128)}, f32[5,1,4,8,4,4]{3,5,4,2,1,0:T(4,128)}, u32[]{:S(2)}, u32[]{:S(2)}) collective-permute-start(f32[5,1,4,8,4,4]{3,5,4,2,1,0:T(4,128)} %get-tuple-element.145), channel_id=1, source_target_pairs={{0,224},{32,0},{64,32},{96,64},{128,96},{160,128},{192,160},{224,1... | collective-permute-start | bytes 30728 | tf_op jit(solution)/shard_map/ppermute | solution.py:115
  51.6 0.8 reshape.333
  52.4 0.8 convert_element_type.38
  53.4 1.5 fusion.29
  54.9 1.1 slice_bitcast_fusion.3
  56.0 0.7 reshape.136
  56.7 0.9 copy.297
  57.6 0.9 copy.302
  58.5 1.1 copy.303
  59.6 1.1 copy.298
  60.8 1.0 broadcast_multiply_fusion
  61.8 1.3 fusion.28
  63.1 1.8 slice_reduce_fusion.2
  65.6 0.7 reshape.332
  66.4 5.6 %multiply_convert_fusion.1 = (bf16[256,4096]{0,1:T(8,128)(2,1)S(1)}, f32[256,4096]{0,1:T(8,128)}) fusion(f32[256]{0:T(256)S(1)} %copy-done.16, f32[5,4096]{1,0:T(8,128)S(1)} %mul.171, f32[5,256]{1,0:T(8,128)S(1)} %copy-done.14), kind=kOutput, calls=%fused_computation.14 | convolution fusion | flops 69206016 | bytes 6379520 | tf_op jit(solution)/shard_map/dot_general | solution.py:36
  72.0 3.8 %multiply_convert_fusion = (bf16[256,4096]{0,1:T(8,128)(2,1)}, f32[256,4096]{0,1:T(8,128)}) fusion(f32[256]{0:T(256)S(1)} %copy-done.17, bf16[256,4096]{0,1:T(8,128)(2,1)S(1)} %get-tuple-element.154, bf16[256,256]{1,0:T(8,128)(2,1)S(1)} %copy-done), kind=kOutput, calls=%fused_computation.12 | convolution fusion | flops 543162368 | bytes 8520704 | tf_op jit(solution)/shard_map/dot_general | solution.py:36
  75.8 2.9 %copy.332 = bf16[256,4096]{1,0:T(8,128)(2,1)S(1)} copy(bf16[256,4096]{0,1:T(8,128)(2,1)} %get-tuple-element.156) | data formatting | bytes 4194304 | tf_op jit(solution)/shard_map/dot_general | solution.py:26
  78.8 4.1 %convert_reduce_fusion = (f32[256]{0:T(256)S(1)}, bf16[256,4096]{0,1:T(8,128)(2,1)S(1)}) fusion(f32[256,4096]{0,1:T(8,128)} %get-tuple-element.157, bf16[5,4096]{1,0:T(8,128)(2,1)} %convert_element_type.38, bf16[256,5]{0,1:T(8,128)(2,1)} %param.29), kind=kOutput, calls=%fused_computation.11 | convolution fusion | flops 22019840 | bytes 6336000 | tf_op jit(solution)/shard_map/dot_general | solution.py:133
  82.9 1.4 fusion.33
  84.4 0.8 copy-done.20
  85.2 4.3 %fusion.32 = (f32[256]{0:T(256)}, f32[256,4096]{0,1:T(8,128)}) fusion(f32[256,4096]{0,1:T(8,128)S(1)} %copy-done.20, bf16[256,4096]{0,1:T(8,128)(2,1)S(1)} %get-tuple-element.161, bf16[256,256]{1,0:T(8,128)(2,1)S(1)} %copy-done), kind=kOutput, calls=%fused_computation.75 | convolution fusion | flops 546307840 | bytes 10617856 | tf_op jit(solution)/shard_map/dot_general | solution.py:137
  89.5 1.5 copy.321
  90.9 0.8 copy.322
  91.7 5.7 %copy.331 = f32[256,4096]{1,0:T(8,128)} copy(f32[256,4096]{0,1:T(8,128)} %get-tuple-element.159) | data formatting | bytes 8388608 | tf_op jit(solution)/shard_map/dot_general | solution.py:26
  97.4 2.2 %fusion.35 = f32[2,128,5]{2,1,0:T(8,128)} fusion(bf16[2,128,4096]{2,1,0:T(8,128)(2,1)S(1)} %bitcast.174, bf16[5,4096,1]{1,0,2:T(8,128)(2,1)} %reshape.333), kind=kOutput, calls=%fused_computation.78 | convolution fusion | flops 10485760 | bytes 2143232 | tf_op jit(solution)/shard_map/dot_general | solution.py:26
  99.6 5.3 %fusion.34 = f32[2,128,5]{2,1,0:T(8,128)S(1)} fusion(f32[2,128,4096]{2,1,0:T(8,128)} %bitcast.169, f32[5,4096,1]{1,0,2:T(8,128)} %reshape.332), kind=kOutput, calls=%fused_computation.77 | convolution fusion | flops 62914560 | bytes 4281344 | tf_op jit(solution)/shard_map/dot_general | solution.py:26
  104.9 0.7 broadcast_in_dim.27
  105.5 1.3 concatenate.40
  106.8 4.0 %collective-permute-start.4 = (f32[128,384]{1,0:T(8,128)S(1)}, f32[128,384]{1,0:T(8,128)S(1)}, u32[]{:S(2)}, u32[]{:S(2)}) collective-permute-start(f32[128,384]{1,0:T(8,128)S(1)} %dynamic-slice_bitcast_fusion), channel_id=1, source_target_pairs={{0,1},{1,0},{2,3},{3,2},{4,5},{5,4},{6,7},{7,6},{8,9},{9,8},{10,11... | collective-permute-start | bytes 589832 | tf_op jit(solution)/shard_map/ppermute | solution.py:84
  110.8 1.0 fusion.25
  111.9 0.8 reshape.138
  112.7 9.7 %all-to-all-start.1 = ((f32[128,1,384]{2,1,0:T(1,128)}), f32[128,1,384]{2,1,0:T(1,128)}, u32[]{:S(2)}, u32[]{:S(2)}) async-start(f32[128,1,384]{2,1,0:T(1,128)} %reshape.138), calls=%async_computation.1 | async-start | bytes 393216 | tf_op jit(solution)/shard_map/all_to_all | solution.py:85
  122.5 1.0 fusion.23
  123.5 5.0 %copy.312 = f32[5,2,4,8,4,4,1]{6,5,4,3,2,1,0:T(4,128)} copy(f32[5,2,4,8,4,4,1]{3,5,4,2,1,0,6:T(4,128)S(1)} %fusion.25) | data formatting | bytes 40960 | tf_op jit(solution)/shard_map/stack | solution.py:49
  128.5 5.0 %copy.311 = f32[5,2,4,8,4,4,1]{6,5,4,3,2,1,0:T(4,128)} copy(f32[5,2,4,8,4,4,1]{3,5,4,2,1,0,6:T(4,128)S(1)} %fusion.23) | data formatting | bytes 40960 | tf_op jit(solution)/shard_map/stack | solution.py:49
  133.6 2.7 %fusion.15 = (f32[5,2,4,8,4,1,4]{3,6,4,2,1,0,5:T(4,128)}, f32[5,2,4,8,1,4,4]{3,6,5,2,1,0,4:T(4,128)}, f32[5,2,4,8,1,4,4]{3,6,5,2,1,0,4:T(4,128)S(1)}, f32[5,2,4,8,4,1,4]{3,6,4,2,1,0,5:T(4,128)S(1)}) fusion(f32[5,2,4,8,4,4,4]{3,6,5,4,2,1,0:T(4,128)S(1)} %bitcast.168, f32[5,2,4,7,4,4]{3,5,4,2,1,0:T(4,128)S(1)} %copy-done.2, ...), kind=kLoop, calls=%fused_computation.33 | loop fusion | flops 61440 | bytes 245760 | tf_op jit(solution)/shard_map/stack | solution.py:49
  136.2 2.0 %copy.305 = f32[5,2,4,8,4,1,4]{6,5,4,3,2,1,0:T(1,128)S(1)} copy(f32[5,2,4,8,4,1,4]{3,6,4,2,1,0,5:T(4,128)} %get-tuple-element.136) | data formatting | bytes 40960 | tf_op jit(solution)/shard_map/stack | solution.py:49
  138.2 2.0 %copy.296 = f32[5,2,4,8,1,4,4]{6,5,4,3,2,1,0:T(4,128)S(1)} copy(f32[5,2,4,8,1,4,4]{3,6,5,2,1,0,4:T(4,128)} %get-tuple-element.137) | data formatting | bytes 40960 | tf_op jit(solution)/shard_map/stack | solution.py:49
  140.2 1.0 copy.295
  141.2 1.1 copy.306
  142.3 1.1 reduce_sum.49
  143.5 0.8 broadcast_in_dim.29
  144.3 13.6 %all-to-all-start.2 = ((f32[128,1,384]{2,1,0:T(1,128)}), f32[128,1,384]{2,1,0:T(1,128)S(1)}, u32[]{:S(2)}, u32[]{:S(2)}) async-start(f32[128,1,384]{2,1,0:T(1,128)} %broadcast_in_dim.29), calls=%async_computation.2 | async-start | bytes 393216 | tf_op jit(solution)/shard_map/all_to_all | solution.py:88
  157.8 6.2 %fusion.7 = f32[5,2,4,8,4,4,4]{6,5,4,3,2,1,0:T(4,128)} fusion(f32[5,2,4,8,1,4,4]{6,5,4,3,2,1,0:T(4,128)S(1)} %copy.296, f32[5,2,4,8,1,4,4]{6,5,4,3,2,1,0:T(4,128)S(1)} %copy.295, f32[5,2,4,8,4,1,4]{6,5,4,3,2,1,0:T(1,128)S(1)} %copy.306, f32[5,2,4,8,4,1,4]{6,5,4,3,2,1,0:T(1,128)S(1)} %copy.305, f32[5,2,4,8,4,4,1]{6,5,4,3,2,1,0:T(4,128)} %copy.312, ...), kind=kLoop, calls=%fused_computation.18 | loop fusion | flops 184320 | bytes 204816 | tf_op jit(solution)/shard_map/mul | solution.py:144
  164.0 4.1 %mul.164 = f32[5,2,4,512]{3,2,1,0:T(4,128)S(1)} reshape(f32[5,2,4,8,4,4,4]{6,5,4,3,2,1,0:T(4,128)} %fusion.7) | data formatting | bytes 163840 | tf_op jit(solution)/shard_map/mul | solution.py:144
  168.1 5.8 %fusion.5 = f32[5,4096]{1,0:T(8,128)S(1)} fusion(f32[256,4096]{0,1:T(8,128)} %get-tuple-element.159, f32[5,256]{1,0:T(8,128)S(1)} %copy-done.14, f32[]{:T(128)S(6)} %rsqrt.3), kind=kOutput, calls=%fused_computation.10 | convolution fusion | flops 62935040 | bytes 4281348 | tf_op jit(solution)/shard_map/dot_general | solution.py:141
  174.0 1.1 collective-permute-start.5
  175.1 0.7 add_add_fusion
  175.7 0.4 collective-permute-done.5
  176.6 0.8 slice_reduce_fusion
  177.4 0.7 slice.215
  178.2 0.7 copy.324
  178.9 0.7 copy.323
  (67 shorter events, 1.2 us)
Async XLA Ops:
  0.6 71.4 %copy-start = (bf16[256,256]{1,0:T(8,128)(2,1)S(1)}, bf16[256,256]{1,0:T(8,128)(2,1)}, u32[]{:S(2)}) copy-start(bf16[256,256]{1,0:T(8,128)(2,1)} %param.27) | copy-start | bytes 393220
  3.6 59.5 %all-to-all-start = ((f32[256,1,128]{2,1,0:T(1,128)}), f32[256,1,128]{2,1,0:T(1,128)}, u32[]{:S(2)}, u32[]{:S(2)}) async-start(f32[256,1,128]{2,1,0:T(1,128)} %broadcast_in_dim.26), calls=%async_computation | async-start | bytes 262144 | tf_op jit(solution)/shard_map/all_to_all | solution.py:74
  26.7 24.9 %copy-start.1 = (f32[2,4,8,5,64]{4,3,2,1,0:T(8,128)S(1)}, f32[2,4,8,5,64]{4,3,2,1,0:T(8,128)}, u32[]{:S(2)}) copy-start(f32[2,4,8,5,64]{4,3,2,1,0:T(8,128)} %fusion.8) | copy-start | bytes 245764
  29.0 81.8 %collective-permute-start.3 = (f32[5,2,1,8,4,4]{3,5,4,1,0,2:T(4,128)}, f32[5,2,1,8,4,4]{3,5,4,1,0,2:T(4,128)}, u32[]{:S(2)}, u32[]{:S(2)}) collective-permute-start(f32[5,2,1,8,4,4]{3,5,4,1,0,2:T(4,128)} %bitcast.26), channel_id=1, source_target_pairs={{0,31},{1,0},{2,1},{3,2},{4,3},{5,4},{6,5},{7,6},{8,7},{9,8},{10,9... | collective-permute-start | bytes 15368 | tf_op jit(solution)/shard_map/ppermute | solution.py:117
  31.2 91.2 %collective-permute-start.2 = (f32[5,2,1,8,4,4]{3,5,4,2,1,0:T(4,128)}, f32[5,2,1,8,4,4]{3,5,4,2,1,0:T(4,128)}, u32[]{:S(2)}, u32[]{:S(2)}) collective-permute-start(f32[5,2,1,8,4,4]{3,5,4,2,1,0:T(4,128)} %bitcast.21), channel_id=1, source_target_pairs={{0,1},{1,2},{2,3},{3,4},{4,5},{5,6},{6,7},{7,8},{8,9},{9,10},{10,1... | collective-permute-start | bytes 15368 | tf_op jit(solution)/shard_map/ppermute | solution.py:116
  32.1 23.9 %copy-start.15 = (s32[2,2,4]{2,1,0:T(2,128)S(1)}, s32[2,2,4]{2,1,0:T(2,128)}, u32[]{:S(2)}) copy-start(s32[2,2,4]{2,1,0:T(2,128)} %param.24) | copy-start | bytes 196
  32.1 101.4 %collective-permute-start = (f32[5,1,4,8,4,4]{3,5,4,2,1,0:T(4,128)}, f32[5,1,4,8,4,4]{3,5,4,2,1,0:T(4,128)}, u32[]{:S(2)}, u32[]{:S(2)}) collective-permute-start(f32[5,1,4,8,4,4]{3,5,4,2,1,0:T(4,128)} %get-tuple-element.144), channel_id=1, source_target_pairs={{0,32},{32,64},{64,96},{96,128},{128,160},{160,192},{192,224},{224... | collective-permute-start | bytes 30728 | tf_op jit(solution)/shard_map/ppermute | solution.py:114
  33.0 100.5 %collective-permute-start.1 = (f32[5,1,4,8,4,4]{3,5,4,2,1,0:T(4,128)}, f32[5,1,4,8,4,4]{3,5,4,2,1,0:T(4,128)}, u32[]{:S(2)}, u32[]{:S(2)}) collective-permute-start(f32[5,1,4,8,4,4]{3,5,4,2,1,0:T(4,128)} %get-tuple-element.145), channel_id=1, source_target_pairs={{0,224},{32,0},{64,32},{96,64},{128,96},{160,128},{192,160},{224,1... | collective-permute-start | bytes 30728 | tf_op jit(solution)/shard_map/ppermute | solution.py:115
  54.9 10.7 %copy-start.12 = (f32[5,2,4,512]{3,2,1,0:T(4,128)S(1)}, f32[5,2,4,512]{3,2,1,0:T(4,128)}, u32[]{:S(2)}) copy-start(f32[5,2,4,512]{3,2,1,0:T(4,128)} %param.21) | copy-start | bytes 245764
  56.0 10.4 %copy-start.14 = (f32[5,256]{1,0:T(8,128)S(1)}, f32[5,256]{1,0:T(8,128)}, u32[]{:S(2)}) copy-start(f32[5,256]{1,0:T(8,128)} %param.25) | copy-start | bytes 15364
  56.0 10.4 %copy-start.16 = (f32[256]{0:T(256)S(1)}, f32[256]{0:T(256)}, u32[]{:S(2)}) copy-start(f32[256]{0:T(256)} %param.26) | copy-start | bytes 3076
  66.4 5.7 %copy-start.17 = (f32[256]{0:T(256)S(1)}, f32[256]{0:T(256)}, u32[]{:S(2)}) copy-start(f32[256]{0:T(256)} %param.28) | copy-start | bytes 3076
  72.0 3.8 %copy-start.18 = (bf16[256,4096]{0,1:T(8,128)(2,1)}, bf16[256,4096]{0,1:T(8,128)(2,1)S(1)}, u32[]{:S(2)}) copy-start(bf16[256,4096]{0,1:T(8,128)(2,1)S(1)} %get-tuple-element.154) | copy-start | bytes 6291460
  78.8 4.2 %copy-start.19 = (bf16[256,4096]{0,1:T(8,128)(2,1)S(1)}, bf16[256,4096]{0,1:T(8,128)(2,1)}, u32[]{:S(2)}) copy-start(bf16[256,4096]{0,1:T(8,128)(2,1)} %copy-done.18) | copy-start | bytes 6291460
  82.9 2.3 %copy-start.20 = (f32[256,4096]{0,1:T(8,128)S(1)}, f32[256,4096]{0,1:T(8,128)}, u32[]{:S(2)}) copy-start(f32[256,4096]{0,1:T(8,128)} %get-tuple-element.155) | copy-start | bytes 12582916
  99.6 6.0 %copy-start.10 = (f32[2,128,1]{2,1,0:T(8,128)S(1)}, f32[2,128,1]{2,1,0:T(8,128)}, u32[]{:S(2)}) copy-start(f32[2,128,1]{2,1,0:T(8,128)} %copy.321) | copy-start | bytes 3076
  99.6 6.0 %copy-start.11 = (f32[2,128,1]{2,1,0:T(8,128)S(1)}, f32[2,128,1]{2,1,0:T(8,128)}, u32[]{:S(2)}) copy-start(f32[2,128,1]{2,1,0:T(8,128)} %copy.322) | copy-start | bytes 3076
  99.6 11.2 %copy-start.7 = (f32[5,2,4,8,4,4,1]{3,6,5,4,2,1,0:T(1,128)S(1)}, f32[5,2,4,8,4,4,1]{3,6,5,4,2,1,0:T(1,128)}, u32[]{:S(2)}) copy-start(f32[5,2,4,8,4,4,1]{3,6,5,4,2,1,0:T(1,128)} %get-tuple-element.135) | copy-start | bytes 61444
  99.6 11.2 %copy-start.9 = (f32[5,2,3,8,4,4,1]{3,6,5,4,2,1,0:T(1,128)S(1)}, f32[5,2,3,8,4,4,1]{3,6,5,4,2,1,0:T(1,128)}, u32[]{:S(2)}) copy-start(f32[5,2,3,8,4,4,1]{3,6,5,4,2,1,0:T(1,128)} %get-tuple-element.133) | copy-start | bytes 46084
  104.8 17.6 %copy-start.6 = (f32[5,2,4,8,4,4,1]{3,6,5,4,2,1,0:T(1,128)S(1)}, f32[5,2,4,8,4,4,1]{3,6,5,4,2,1,0:T(1,128)}, u32[]{:S(2)}) copy-start(f32[5,2,4,8,4,4,1]{3,6,5,4,2,1,0:T(1,128)} %get-tuple-element.134) | copy-start | bytes 61444
  104.8 17.6 %copy-start.8 = (f32[5,2,3,8,4,4,1]{3,6,5,4,2,1,0:T(1,128)S(1)}, f32[5,2,3,8,4,4,1]{3,6,5,4,2,1,0:T(1,128)}, u32[]{:S(2)}) copy-start(f32[5,2,3,8,4,4,1]{3,6,5,4,2,1,0:T(1,128)} %get-tuple-element.132) | copy-start | bytes 46084
  106.8 5.0 %collective-permute-start.4 = (f32[128,384]{1,0:T(8,128)S(1)}, f32[128,384]{1,0:T(8,128)S(1)}, u32[]{:S(2)}, u32[]{:S(2)}) collective-permute-start(f32[128,384]{1,0:T(8,128)S(1)} %dynamic-slice_bitcast_fusion), channel_id=1, source_target_pairs={{0,1},{1,0},{2,3},{3,2},{4,5},{5,4},{6,7},{7,6},{8,9},{9,8},{10,11... | collective-permute-start | bytes 589832 | tf_op jit(solution)/shard_map/ppermute | solution.py:84
  112.7 29.6 %all-to-all-start.1 = ((f32[128,1,384]{2,1,0:T(1,128)}), f32[128,1,384]{2,1,0:T(1,128)}, u32[]{:S(2)}, u32[]{:S(2)}) async-start(f32[128,1,384]{2,1,0:T(1,128)} %reshape.138), calls=%async_computation.1 | async-start | bytes 393216 | tf_op jit(solution)/shard_map/all_to_all | solution.py:85
  123.5 10.0 %copy-start.2 = (f32[5,2,4,7,4,4]{3,5,4,2,1,0:T(4,128)S(1)}, f32[5,2,4,7,4,4]{3,5,4,2,1,0:T(4,128)}, u32[]{:S(2)}) copy-start(f32[5,2,4,7,4,4]{3,5,4,2,1,0:T(4,128)} %get-tuple-element.142) | copy-start | bytes 53764
  123.5 10.0 %copy-start.3 = (f32[5,2,4,7,4,4]{3,5,4,2,1,0:T(4,128)S(1)}, f32[5,2,4,7,4,4]{3,5,4,2,1,0:T(4,128)}, u32[]{:S(2)}) copy-start(f32[5,2,4,7,4,4]{3,5,4,2,1,0:T(4,128)} %get-tuple-element.143) | copy-start | bytes 53764
  123.5 10.0 %copy-start.4 = (f32[5,2,4,1,4,4]{3,5,4,2,1,0:T(4,128)S(1)}, f32[5,2,4,1,4,4]{3,5,4,2,1,0:T(4,128)}, u32[]{:S(2)}) copy-start(f32[5,2,4,1,4,4]{3,5,4,2,1,0:T(4,128)} %get-tuple-element.162) | copy-start | bytes 7684
  123.5 10.0 %copy-start.5 = (f32[5,2,4,1,4,4]{3,5,4,2,1,0:T(4,128)S(1)}, f32[5,2,4,1,4,4]{3,5,4,2,1,0:T(4,128)}, u32[]{:S(2)}) copy-start(f32[5,2,4,1,4,4]{3,5,4,2,1,0:T(4,128)} %get-tuple-element.163) | copy-start | bytes 7684
  144.3 29.7 %all-to-all-start.2 = ((f32[128,1,384]{2,1,0:T(1,128)}), f32[128,1,384]{2,1,0:T(1,128)S(1)}, u32[]{:S(2)}, u32[]{:S(2)}) async-start(f32[128,1,384]{2,1,0:T(1,128)} %broadcast_in_dim.29), calls=%async_computation.2 | async-start | bytes 393216 | tf_op jit(solution)/shard_map/all_to_all | solution.py:88
  168.1 7.0 %copy-start.13 = (f32[5,2,4,512]{3,2,1,0:T(4,128)S(1)}, f32[5,2,4,512]{3,2,1,0:T(4,128)}, u32[]{:S(2)}) copy-start(f32[5,2,4,512]{3,2,1,0:T(4,128)} %reshape.136) | copy-start | bytes 245764
  174.0 2.1 %collective-permute-start.5 = (f32[128,1,384]{2,1,0:T(1,128)S(1)}, f32[128,1,384]{2,1,0:T(1,128)S(1)}, u32[]{:S(2)}, u32[]{:S(2)}) collective-permute-start(f32[128,1,384]{2,1,0:T(1,128)S(1)} %all-to-all-done.2), channel_id=1, source_target_pairs={{0,1},{1,0},{2,3},{3,2},{4,5},{5,4},{6,7},{7,6},{8,9},{9,8},{10,11... | collective-permute-start | bytes 589832 | tf_op jit(solution)/shard_map/ppermute | solution.py:92

commit v2 on v1

v2 whole, which is shorter than its diff:
```python
import functools
import math

import jax
import jax.numpy as jnp
from jax import lax
from jax.experimental import pallas as pl
from jax.experimental.pallas import tpu as pltpu
from jax.sharding import Mesh, PartitionSpec as P

KAPPA = 0.5
DT_STEP = 0.5
EPS = 1e-06

AXES = ("zhi", "y", "x", "zlo", "core")
GX = ("zhi", "y")
GZ = ("x", "zlo", "core")
CHIPS = ("zhi", "y", "x", "zlo")
LANES = 128
NODES = 64
GROUP = 8
F32 = jnp.float32
BF16 = jnp.bfloat16


def whole_vmem(count):
    return [pl.BlockSpec(memory_space=pltpu.VMEM)] * count


def rows_of(ref, *lead):
    return jnp.concatenate([ref[lead + (0,)], ref[lead + (1,)]], axis=0)


def adjoint_kernel(
    state_ref, cot_ref, inv_ref, w_mid_ref, b_mid_ref,
    adj_ref, og_ref, xs_ref, w_mid_t_ref, b_col_ref, left_ref, right_ref, front_ref, back_ref,
    rows_ref,
):
    channels, _, span, line = state_ref.shape
    tiles = line // LANES
    cells = 2 * span
    cots = []
    for c in range(channels):
        full = rows_of(cot_ref, c)
        cots.append([full[:, q * LANES : (q + 1) * LANES] for q in range(tiles)])
    lane = lax.broadcasted_iota(jnp.int32, (cells, LANES), 1)
    base = lane - lax.rem(lane, NODES)

    def step(n, acc):
        index = base + n
        slab = rows_of(inv_ref, n)
        out = []
        for c in range(channels):
            for q in range(tiles):
                spread = jnp.take_along_axis(cots[c][q], index, axis=1, mode="promise_in_bounds")
                out.append(acc[c * tiles + q] + slab[:, q * LANES : (q + 1) * LANES] * spread)
        return tuple(out)

    zero = jnp.zeros((cells, LANES), F32)
    acc = lax.fori_loop(0, NODES, step, (zero,) * (channels * tiles), unroll=4)
    ones = jnp.ones((cells, line), F32)
    blank = jnp.zeros((cells, line), F32)

    def fill(get):
        for r in range(GROUP):
            value = get(r) if r < channels else (ones if r == channels else blank)
            for q in range(tiles):
                rows_ref[q, pl.ds(r, cells, stride=GROUP), :] = value[:, q * LANES : (q + 1) * LANES]

    def tile_of(t):
        return jnp.concatenate([rows_ref[q, t * GROUP : (t + 1) * GROUP, :] for q in range(tiles)], axis=1)

    adjoint = [jnp.concatenate(acc[c * tiles : (c + 1) * tiles], axis=1) for c in range(channels)]
    for c in range(channels):
        adj_ref[c] = adjoint[c]
        left_ref[c] = adjoint[c][:span]
        right_ref[c] = adjoint[c][span:]
        front_ref[c] = jnp.concatenate([adjoint[c][0:1], adjoint[c][span : span + 1]], axis=0)
        back_ref[c] = jnp.concatenate([adjoint[c][span - 1 : span], adjoint[c][cells - 1 :]], axis=0)
    fill(lambda r: DT_STEP * adjoint[r])
    for t in range(cells):
        tile = tile_of(t)
        og_ref[t] = jnp.concatenate([tile, blank], axis=0).astype(BF16)
    fill(lambda r: rows_of(state_ref, r))
    for t in range(cells):
        tile = tile_of(t)
        high = tile.astype(BF16).astype(F32)
        xs_ref[t] = jnp.concatenate([high, tile - high, high, blank], axis=0).astype(BF16)
    w_mid_t_ref[...] = w_mid_ref[...].astype(F32).T.astype(BF16)
    b_col_ref[...] = jnp.broadcast_to(b_mid_ref[...], (LANES, b_mid_ref.shape[1])).T


def dot(a, b):
    return jnp.dot(a, b, preferred_element_type=F32)


def dot_nt(a, b):
    return lax.dot_general(a, b, (((1,), (1,)), ((), ())), preferred_element_type=F32)


def sigmoid(v):
    return 0.5 * jnp.tanh(0.5 * v) + 0.5


def closure_kernel(
    entries,
    core_ref, squares_ref, xs_ref, og_ref, w_in_ref, b_in_ref, w_mid_ref, w_mid_t_ref, b_col_ref, w_out_ref,
    back_ref, mine_ref, other_ref,
    mid_ref, in_ref, out_ref,
):
    cells = xs_ref.shape[0]
    channels, hidden = w_in_ref.shape
    total = jnp.sum(squares_ref[...], axis=0, keepdims=True)
    inv_norm = lax.rsqrt(total / entries + EPS)[:, :1]
    weights = jnp.concatenate(
        [inv_norm * w_in_ref[...], b_in_ref[...], jnp.zeros((GROUP - channels - 1, hidden), F32)], axis=0
    )
    high = weights.astype(BF16).astype(F32)
    low = weights - high
    pair = jnp.concatenate([high, low], axis=0).astype(BF16)
    first = jnp.concatenate([high, high, low, jnp.zeros_like(low)], axis=0).T.astype(BF16)
    mid_ref[...] = jnp.zeros_like(mid_ref)
    in_ref[...] = jnp.zeros_like(in_ref)
    out_ref[...] = jnp.zeros_like(out_ref)

    def step(t, carry):
        x = xs_ref[t]
        og = og_ref[t]
        pre_first = dot(first, x)
        gate = sigmoid(pre_first)
        act = pre_first * gate
        slope_one = gate + act * (1.0 - gate)
        hidden_one = act.astype(BF16)
        pre_second = dot(w_mid_t_ref[...], hidden_one) + b_col_ref[:, :1]
        gate = sigmoid(pre_second)
        act = pre_second * gate
        slope_two = gate + act * (1.0 - gate)
        hidden_two = act.astype(BF16)
        delta_two = (dot(w_out_ref[...], og) * slope_two).astype(BF16)
        delta_one = (dot(w_mid_ref[...], delta_two) * slope_one).astype(BF16)
        mid_ref[...] += dot_nt(jnp.concatenate([hidden_one, og], axis=0), delta_two)
        out_ref[...] += dot_nt(og, hidden_two)
        in_ref[...] += dot_nt(x[: 2 * GROUP], delta_one)
        back = dot(pair, delta_one)
        back = back[:GROUP] + back[GROUP:]
        place = pl.ds(pl.multiple_of(t * GROUP, GROUP), GROUP)
        for q in range(back_ref.shape[0]):
            back_ref[q, place, :] = back[:, q * LANES : (q + 1) * LANES]
        return carry

    lax.fori_loop(0, cells, step, 0)
    c = channels
    sums = in_ref[...]
    extra = jnp.concatenate(
        [
            (sums[:c] + sums[GROUP : GROUP + c]) * inv_norm,
            sums[c : c + 1],
            jnp.zeros((GROUP - c - 1, hidden), F32),
            out_ref[:c],
            mid_ref[hidden + c : hidden + c + 1],
            jnp.zeros((GROUP - c - 1, hidden), F32),
        ],
        axis=0,
    )
    half = hidden // 2
    wide = jnp.concatenate([extra[:, :half], extra[:, half:]], axis=0)
    wide = jnp.concatenate([wide, jnp.zeros((half - wide.shape[0], half), F32)], axis=0)
    core = core_ref[0]
    own = pl.multiple_of(core * half, half)
    away = pl.multiple_of((1 - core) * half, half)
    mine_ref[:, 0, :hidden] = mid_ref[pl.ds(own, half), :]
    other_ref[:, 0, :hidden] = mid_ref[pl.ds(away, half), :]
    first_half = core == 0
    mine_ref[:, 0, hidden:] = jnp.where(first_half, wide, 0.0)
    other_ref[:, 0, hidden:] = jnp.where(first_half, 0.0, wide)


def finish_kernel(
    tags_ref, adj_ref, back_ref, left_ref, right_ref, front_ref, rear_ref, out_ref
):
    channels, cells, line = adj_ref.shape
    span = cells // 2
    lane = lax.broadcasted_iota(jnp.int32, (cells, line), 1)
    row = lax.broadcasted_iota(jnp.int32, (cells, line), 0)
    node = lax.rem(lane, NODES)
    a, b, c3 = node // 16, lax.rem(node // 4, 4), lax.rem(node, 4)
    bottom = jnp.zeros((cells, line), F32)
    top = jnp.zeros((cells, line), F32)
    for r in range(cells):
        bottom = jnp.where(row == r, 1.0 - 2.0 * tags_ref[0, r].astype(F32), bottom)
        top = jnp.where(row == r, 1.0 - 2.0 * tags_ref[1, r].astype(F32), top)
    low_wall = lane < NODES
    high_wall = lane >= line - NODES
    for c in range(channels):
        v = adj_ref[c]
        lx = jnp.concatenate([left_ref[c], v[:span]], axis=0)
        ux = jnp.concatenate([v[span:], right_ref[c]], axis=0)
        lz = jnp.concatenate([front_ref[c, 0:1], v[: span - 1], front_ref[c, 1:2], v[span : cells - 1]], axis=0)
        uz = jnp.concatenate([v[1:span], rear_ref[c, 0:1], v[span + 1 :], rear_ref[c, 1:2]], axis=0)
        ly = jnp.where(low_wall, bottom * v, pltpu.roll(v, 52, 1))
        uy = jnp.where(high_wall, top * v, pltpu.roll(v, line - 52, 1))
        jump = jnp.where(a == 0, pltpu.roll(lx, line - 48, 1) - v, 0.0)
        jump += jnp.where(a == 3, pltpu.roll(ux, 48, 1) - v, 0.0)
        jump += jnp.where(b == 0, ly - v, 0.0)
        jump += jnp.where(b == 3, uy - v, 0.0)
        jump += jnp.where(c3 == 0, pltpu.roll(lz, line - 3, 1) - v, 0.0)
        jump += jnp.where(c3 == 3, pltpu.roll(uz, 3, 1) - v, 0.0)
        back = jnp.concatenate(
            [back_ref[q, pl.ds(c, cells, stride=GROUP), :] for q in range(line // LANES)], axis=1
        )
        total = v + (0.5 * KAPPA) * jump + back
        out_ref[c, 0] = total[:span]
        out_ref[c, 1] = total[span:]


def shape(*dims, dtype=F32):
    return jax.ShapeDtypeStruct(dims, dtype)


def run_adjoint(state, cotangent, local_inverse, w_mid, b_mid):
    channels, _, span, line = state.shape
    cells = 2 * span
    hidden = w_mid.shape[0]
    return pl.pallas_call(
        adjoint_kernel,
        out_shape=(
            shape(channels, cells, line),
            shape(cells, 2 * GROUP, line, dtype=BF16),
            shape(cells, 4 * GROUP, line, dtype=BF16),
            shape(hidden, hidden, dtype=BF16),
            shape(hidden, LANES),
            shape(channels, span, line),
            shape(channels, span, line),
            shape(channels, 2, line),
            shape(channels, 2, line),
        ),
        in_specs=whole_vmem(5),
        out_specs=tuple(whole_vmem(9)),
        scratch_shapes=[pltpu.VMEM((line // LANES, cells * GROUP, LANES), F32)],
        name="adjoint",
    )(state, cotangent, local_inverse, w_mid, b_mid.reshape(1, hidden))


def run_closure(entries, core, squares, xs, og, w_in, b_in, w_mid, w_mid_t, b_col, w_out):
    cells, _, line = xs.shape
    channels, hidden = w_in.shape
    half = hidden // 2
    return pl.pallas_call(
        functools.partial(closure_kernel, entries),
        out_shape=(
            shape(line // LANES, cells * GROUP, LANES),
            shape(half, 1, hidden + LANES),
            shape(half, 1, hidden + LANES),
        ),
        in_specs=[pl.BlockSpec(memory_space=pltpu.SMEM)] + whole_vmem(9),
        out_specs=tuple(whole_vmem(3)),
        scratch_shapes=[
            pltpu.VMEM((hidden + 2 * GROUP, hidden), F32),
            pltpu.VMEM((2 * GROUP, hidden), F32),
            pltpu.VMEM((2 * GROUP, hidden), F32),
        ],
        name="closure",
    )(core, squares, xs, og, w_in, b_in.reshape(1, hidden), w_mid, w_mid_t, b_col, w_out)


def run_finish(tags, adjoint, back, left, right, front, rear):
    channels, cells, line = adjoint.shape
    return pl.pallas_call(
        finish_kernel,
        out_shape=shape(channels, 2, cells // 2, line),
        in_specs=[pl.BlockSpec(memory_space=pltpu.SMEM)] + whole_vmem(6),
        out_specs=pl.BlockSpec(memory_space=pltpu.VMEM),
        name="finish",
    )(tags, adjoint, back, left, right, front, rear)


def ring(count, step):
    return [(i, (i + step) % count) for i in range(count)]


def exchange(value, axes):
    return lax.all_to_all(value, axes, 0, 0, tiled=True)


def per_device(state, cotangent, local_inverse, wall_tags, w_in, b_in, w_mid, b_mid, w_out):
    channels, x_elems, z_elems, line = state.shape
    gx, gz = lax.axis_size(GX), lax.axis_size(GZ)
    devices = gx * gz
    chips = devices // 2
    nodes = x_elems * z_elems * line * devices
    hidden = w_mid.shape[0]
    swap = [(0, 1), (1, 0)]
    core = lax.axis_index("core")

    squares = jnp.broadcast_to(jnp.sum(state * state), (devices, 1, LANES))
    squares = exchange(squares, AXES).reshape(devices, LANES)
    adjoint, og, xs, w_mid_t, b_col, low_x, high_x, low_z, high_z = run_adjoint(
        state, cotangent, local_inverse, w_mid, b_mid
    )
    from_left = lax.ppermute(high_x, GX, ring(gx, 1))
    from_right = lax.ppermute(low_x, GX, ring(gx, -1))
    from_front = lax.ppermute(high_z, GZ, ring(gz, 1))
    from_rear = lax.ppermute(low_z, GZ, ring(gz, -1))
    w_out_wide = jnp.pad(w_out, ((0, 0), (0, 2 * GROUP - channels)))
    back, mine, other = run_closure(
        float(channels * nodes), core.reshape(1), squares, xs, og, w_in, b_in, w_mid, w_mid_t, b_col, w_out_wide
    )
    mine = mine + lax.ppermute(other, "core", swap)
    factor = 4.0 / math.sqrt(nodes)
    chunk = factor * jnp.sum(exchange(mine, CHIPS), axis=0, keepdims=True)
    gathered = exchange(jnp.broadcast_to(chunk, (chips,) + chunk.shape[1:]), CHIPS)
    partner = lax.ppermute(gathered, "core", swap)
    grad_state = run_finish(
        wall_tags.reshape(2, x_elems * z_elems), adjoint, back, from_left, from_right, from_front, from_rear
    )
    gathered, partner = gathered[:, 0], partner[:, 0]
    first = jnp.where(core == 0, gathered, partner)
    second = jnp.where(core == 0, partner, gathered)
    grad_mid = jnp.concatenate([first[:, :hidden], second[:, :hidden]], axis=0)
    extra = jnp.concatenate([first[: 2 * GROUP, hidden:], first[2 * GROUP : 4 * GROUP, hidden:]], axis=1)
    c = channels
    return (
        grad_state,
        extra[:c],
        extra[c],
        grad_mid,
        extra[GROUP + c],
        extra[GROUP : GROUP + c].T,
    )


def solution(mesh):
    fine = Mesh(mesh.devices.reshape(2, 4, 4, 4, 2), AXES)
    block = P(None, GX, GZ, None)
    placed = (block, block, block, P(None, GX, GZ)) + (P(),) * 5
    return jax.shard_map(
        per_device,
        mesh=fine,
        in_specs=placed,
        out_specs=(block, P(), P(), P(), P(), P()),
        check_vma=False,
    )
```

time: 182 us -> 107 us (0.59)
  local copies, waits for them, and re-layouts: 57 us -> 6.43 us
  starting transfers between devices: 66.6 us -> 28.3 us
  blocking collectives: 0 us -> 38.1 us
  matrix products: 36.2 us -> 0 us
  Pallas kernels: 0 us -> 16.9 us
  other arithmetic: 17.5 us -> 5.02 us
  waiting for transfers between devices: 0.46 us -> 10.1 us
    all_to_all x0 -> x2, blocking collectives: none -> 38.1 us  [exchange(): return lax.all_to_all(value, axes, 0, 0, tiled=True)]
    dot_general x9 -> x0, matrix products: 36.2 us -> none  [the longest x2 9.45 us: inner_first(): lax.dot_general(first_op, second_op, (((0,), (0,)), ((), ())), precision=...]
    all_to_all x3 -> x1, starting transfers between devices: 39.9 us -> 15.6 us  [exchange(): return lax.all_to_all(value, axes, 0, 0, tiled=True)]
    another operation x9 -> x0, local copies, waits for them, and re-layouts: 17.6 us -> none  [the longest x8 16.1 us: face_terms(): jnp.stack([lower_term, zero_face, zero_face, upper_term], axis=face_axis)]
    pallas_call x0 -> x3, Pallas kernels: none -> 16.9 us  [the longest x1 10 us: run_closure(): pl.pallas_call(functools.partial(closure_kernel, entries), out_shape=(sha...]
    ppermute x6, starting transfers between devices: 26.7 us -> 12.6 us  [the longest x1 7.36 us: per_device(): from_right = lax.ppermute(low_x, GX, ring(gx, -1))]
    dot_general x2 -> x0, local copies, waits for them, and re-layouts: 8.56 us -> none  [inner_rows(): lax.dot_general(first_op, second_op, (((1,), (1,)), ((), ())), precision=...]
    mul x4 -> x1, other arithmetic: 7.19 us -> 0.01 us  [per_device(): chunk = factor * jnp.sum(exchange(mine, CHIPS), axis=0, keepdims=True)]
  transfers between devices with their start and end apart: 9 -> 7, of which waited for: 1 -> 4; matrix products, arithmetic and copies ran while one was open for 56% -> 1% of each run, Pallas kernels for 0% -> 7%
where the time goes in v2:
time: 107 us; the launch traced here: 106 us
  blocking collectives  38.1 us (36%)
  starting transfers between devices  28.3 us (26%)
  Pallas kernels  16.9 us (16%)
  waiting for transfers between devices  10.1 us (9%)
  local copies, waits for them, and re-layouts  6.43 us (6%)
  other arithmetic  5.02 us (5%)
    all_to_all x2, blocking collectives, exchange(): return lax.all_to_all(value, axes, 0, 0, tiled=True)  38.1 us
    all_to_all x1, starting transfers between devices, exchange(): return lax.all_to_all(value, axes, 0, 0, tiled=True)  15.6 us
    pallas_call x1, Pallas kernels, run_closure(): pl.pallas_call(functools.partial(closure_kernel, entries), out_shape=(sha...  10 us
    ppermute x1, starting transfers between devices, per_device(): from_right = lax.ppermute(low_x, GX, ring(gx, -1))  7.36 us
    all_to_all x1, waiting for transfers between devices, exchange(): return lax.all_to_all(value, axes, 0, 0, tiled=True)  6.24 us
    pallas_call x1, Pallas kernels, run_adjoint(): pl.pallas_call(adjoint_kernel, out_shape=(shape(channels, cells, line), s...  5.05 us
    unnamed x26, local copies, waits for them, and re-layouts  2.77 us
    ppermute x1, starting transfers between devices, per_device(): partner = lax.ppermute(gathered, 'core', swap)  2.59 us
  transfers between devices with their start and end apart: 7, of which 4 were waited for; matrix products, arithmetic and copies ran while one was open for 1% of the time, Pallas kernels for 7%

profile of v2, /device:TPU:1, one launch (start us, length us, event | category | flops | bytes accessed | tf_op | source)
XLA Modules:
  0.0 105.5 jit_solution(16014940594281900893)
XLA Ops:
  0.6 1.5 %multiply_reduce_fusion = f32[]{:T(128)} fusion(f32[5,2,4,512]{3,2,1,0:T(4,128)} %state_ref.1), kind=kLoop, calls=%fused_computation.4 | loop fusion | flops 40959 | bytes 81924 | tf_op jit(solution)/shard_map/reduce_sum | solution.py:295
  2.2 1.4 %broadcast_in_dim.4 = f32[256,1,128]{2,1,0:T(1,128)} broadcast(f32[]{:T(128)} %multiply_reduce_fusion), dimensions={} | broadcast | bytes 131076 | tf_op jit(solution)/shard_map/broadcast_in_dim | solution.py:295
  3.5 15.6 %all-to-all-start = ((f32[256,1,128]{2,1,0:T(1,128)}), f32[256,1,128]{2,1,0:T(1,128)S(1)}, u32[]{:S(2)}, u32[]{:S(2)}) async-start(f32[256,1,128]{2,1,0:T(1,128)} %broadcast_in_dim.4), calls=%async_computation | async-start | bytes 262144 | tf_op jit(solution)/shard_map/all_to_all | solution.py:282
  19.2 0.0 copy-start.6
  19.2 0.7 copy-done.6
  19.9 0.1 copy.16
  20.0 0.6 pad.4.w_out_ref
  20.7 5.1 %adjoint.1 = (f32[5,8,512]{2,1,0:T(8,128)}, bf16[8,16,512]{2,1,0:T(8,128)(2,1)}, bf16[8,32,512]{2,1,0:T(8,128)(2,1)}, bf16[256,256]{1,0:T(8,128)(2,1)}, f32[256,...) custom-call(f32[5,2,4,512]{3,2,1,0:T(4,128)} %state_ref.1, ...), custom_call_target="tpu_custom_call" | custom-call | tf_op jit(solution)/shard_map/adjoint/pallas_call | solution.py:224
  25.7 6.2 %all-to-all-done = f32[256,1,128]{2,1,0:T(1,128)S(1)} async-done(((f32[256,1,128]{2,1,0:T(1,128)}), f32[256,1,128]{2,1,0:T(1,128)S(1)}, u32[]{:S(2)}, u32[]{:S(2)}) %all-to-all-start) | async-done | bytes 131104 | tf_op jit(solution)/shard_map/all_to_all | solution.py:282
  32.0 0.0 copy-start.1
  32.0 0.6 copy-done.1
  32.6 10.0 %closure.1 = (f32[4,64,128]{2,1,0:T(8,128)}, f32[128,1,384]{2,1,0:T(1,128)}, f32[128,1,384]{2,1,0:T(1,128)}) custom-call(s32[1]{0:T(128)} %bitcast.1.core_ref, f32[256,128]{1,0:T(8,128)} %bitcast.14, bf16[8,32,512]{2,1,0:T(8,128)(2,1)} %get-tuple-element.19.xs_ref, bf16[8,16,512]{2,1,0:T(8,128)(2,1)} %get-tuple-element.20.og_ref, f32[5,256]{1,0:T(8,128)} %w_in_ref.1, ...), custom_call_target="tpu_custom_call" | custom-call | tf_op jit(solution)/shard_map/closure/pallas_call | solution.py:248
  42.6 1.0 collective-permute-start.4
  43.6 1.3 %collective-permute-done.4 = f32[128,1,384]{2,1,0:T(1,128)S(1)} collective-permute-done((f32[128,1,384]{2,1,0:T(1,128)}, f32[128,1,384]{2,1,0:T(1,128)S(1)}, u32[]{:S(2)}, u32[]{:S(2)}) %collective-permute-start.4) | collective-permute-done | bytes 196640 | tf_op jit(solution)/shard_map/ppermute | solution.py:308
  44.9 1.1 %add.5 = f32[128,1,384]{2,1,0:T(1,128)S(1)} add(f32[128,1,384]{2,1,0:T(1,128)} %get-tuple-element.28, f32[128,1,384]{2,1,0:T(1,128)S(1)} %collective-permute-done.4) | non-fusion elementwise | flops 49152 | bytes 589824 | tf_op jit(solution)/shard_map/add | solution.py:308
  46.0 20.3 %all_to_all.15 = f32[128,1,384]{2,1,0:T(1,128)S(1)} all-to-all(f32[128,1,384]{2,1,0:T(1,128)S(1)} %add.5), channel_id=1, replica_groups=mesh['zhi'=2,'y'=4,'x'=4,'zlo'=4,'core'=2] {'zhi','y','x','zlo'}, dimensions={0} | all-to-all | bytes 393216 | tf_op jit(solution)/shard_map/all_to_all | solution.py:282
  66.3 0.2 reduce_sum.19
  66.5 0.1 broadcast_in_dim.10
  66.6 17.7 %all_to_all.16 = f32[128,1,384]{2,1,0:T(1,128)S(1)} all-to-all(f32[128,1,384]{2,1,0:T(1,128)S(1)} %broadcast_in_dim.10), channel_id=1, replica_groups=mesh['zhi'=2,'y'=4,'x'=4,'zlo'=4,'core'=2] {'zhi','y','x','zlo'}, dimensions={0} | all-to-all | bytes 393216 | tf_op jit(solution)/shard_map/all_to_all | solution.py:282
  84.4 0.0 copy-start.9
  84.4 0.0 copy-start.8
  84.4 0.0 copy-start.11
  84.4 0.0 copy-start.10
  84.4 2.6 %collective-permute-start.5 = (f32[128,1,384]{2,0,1:T(8,128)S(1)}, f32[128,1,384]{2,0,1:T(8,128)S(1)}, u32[]{:S(2)}, u32[]{:S(2)}) collective-permute-start(f32[128,1,384]{2,0,1:T(8,128)S(1)} %copy.18), channel_id=1, source_target_pairs={{0,1},{1,0},{2,3},{3,2},{4,5},{5,4},{6,7},{7,6},{8,9},{9,8},{10,11... | collective-permute-start | bytes 589832 | tf_op jit(solution)/shard_map/ppermute | solution.py:312
  87.0 0.0 copy-done.9
  87.0 0.1 collective-permute-start
  87.1 0.0 copy-done.8
  87.1 7.4 %collective-permute-start.1 = (f32[5,4,512]{2,1,0:T(4,128)S(1)}, f32[5,4,512]{2,1,0:T(4,128)S(1)}, u32[]{:S(2)}, u32[]{:S(2)}) collective-permute-start(f32[5,4,512]{2,1,0:T(4,128)S(1)} %copy-done.8), channel_id=1, source_target_pairs={{0,224},{32,0},{64,32},{96,64},{128,96},{160,128},{192,160},{224,1... | collective-permute-start | bytes 122888 | tf_op jit(solution)/shard_map/ppermute | solution.py:301
  94.5 0.0 copy-done.11
  94.5 0.0 copy-start.7
  94.5 1.6 %collective-permute-start.2 = (f32[5,2,512]{2,1,0:T(2,128)S(1)}, f32[5,2,512]{2,1,0:T(2,128)S(1)}, u32[]{:S(2)}, u32[]{:S(2)}) collective-permute-start(f32[5,2,512]{2,1,0:T(2,128)S(1)} %copy-done.11), channel_id=1, source_target_pairs={{0,1},{1,2},{2,3},{3,4},{4,5},{5,6},{6,7},{7,8},{8,9},{9,10},{10,1... | collective-permute-start | bytes 61448 | tf_op jit(solution)/shard_map/ppermute | solution.py:302
  96.1 0.0 copy-done.10
  96.1 0.0 collective-permute-start.3
  96.1 0.0 copy-done.7
  96.1 0.6 reshape.40.tags_ref
  96.7 0.3 collective-permute-done.2.front_ref
  97.0 0.0 copy-start.4
  97.0 2.3 %collective-permute-done.3.rear_ref = f32[5,2,512]{2,1,0:T(2,128)S(1)} collective-permute-done((f32[5,2,512]{2,1,0:T(2,128)S(1)}, f32[5,2,512]{2,1,0:T(2,128)S(1)}, u32[]{:S(2)}, u32[]{:S(2)}) %collective-permute-start.3) | collective-permute-done | bytes 20512 | tf_op jit(solution)/shard_map/ppermute | solution.py:303
  99.3 0.0 copy-start.5
  99.3 0.0 collective-permute-done.left_ref
  99.3 0.0 copy-start.2
  99.3 0.0 collective-permute-done.1.right_ref
  99.3 0.0 copy-start.3
  99.3 0.0 copy-done.4
  99.3 0.6 copy-done.5
  99.9 0.0 copy-done.2
  99.9 0.0 copy-done.3
  99.9 1.8 %finish.1 = f32[5,2,4,512]{3,2,1,0:T(4,128)} custom-call(s32[2,8]{1,0:T(2,128)} %reshape.40.tags_ref, f32[5,8,512]{2,1,0:T(8,128)} %get-tuple-element.18.adj_ref, f32[4,64,128]{2,1,0:T(8,128)} %get-tuple-element.23.back_ref, f32[5,4,512]{2,1,0:T(4,128)} %copy-done.2, f32[5,4,512]{2,1,0:T(4,128)} %copy-done.3, f32[5,2,512]{2,1,0:T(2,128)} %copy-done.4, ...), custom_call_target="tpu_custom_call" | custom-call | tf_op jit(solution)/shard_map/finish/pallas_call | solution.py:268
  101.7 0.0 collective-permute-done.5
  101.8 0.0 copy-start
  101.8 0.7 copy-done
  102.5 0.6 fusion.2
  103.0 0.6 fusion.1
  103.6 0.3 broadcast_select_fusion
  103.9 0.0 slice-start
  103.9 0.9 slice-done
  104.8 0.7 pad_maximum_fusion
  (6 shorter events, 0.1 us)
Async XLA Ops:
  3.5 28.4 %all-to-all-start = ((f32[256,1,128]{2,1,0:T(1,128)}), f32[256,1,128]{2,1,0:T(1,128)S(1)}, u32[]{:S(2)}, u32[]{:S(2)}) async-start(f32[256,1,128]{2,1,0:T(1,128)} %broadcast_in_dim.4), calls=%async_computation | async-start | bytes 262144 | tf_op jit(solution)/shard_map/all_to_all | solution.py:282
  19.2 0.7 copy-start.6
  32.0 0.6 copy-start.1
  42.6 2.3 %collective-permute-start.4 = (f32[128,1,384]{2,1,0:T(1,128)}, f32[128,1,384]{2,1,0:T(1,128)S(1)}, u32[]{:S(2)}, u32[]{:S(2)}) collective-permute-start(f32[128,1,384]{2,1,0:T(1,128)} %get-tuple-element.29), channel_id=1, source_target_pairs={{0,1},{1,0},{2,3},{3,2},{4,5},{5,4},{6,7},{7,6},{8,9},{9,8},{10,11... | collective-permute-start | bytes 589832 | tf_op jit(solution)/shard_map/ppermute | solution.py:308
  84.4 2.6 %copy-start.9 = (f32[5,4,512]{2,1,0:T(4,128)S(1)}, f32[5,4,512]{2,1,0:T(4,128)}, u32[]{:S(2)}) copy-start(f32[5,4,512]{2,1,0:T(4,128)} %get-tuple-element.24) | copy-start | bytes 122884
  84.4 2.7 %copy-start.8 = (f32[5,4,512]{2,1,0:T(4,128)S(1)}, f32[5,4,512]{2,1,0:T(4,128)}, u32[]{:S(2)}) copy-start(f32[5,4,512]{2,1,0:T(4,128)} %get-tuple-element.25) | copy-start | bytes 122884
  84.4 10.1 %copy-start.11 = (f32[5,2,512]{2,1,0:T(2,128)S(1)}, f32[5,2,512]{2,1,0:T(2,128)}, u32[]{:S(2)}) copy-start(f32[5,2,512]{2,1,0:T(2,128)} %get-tuple-element.26) | copy-start | bytes 61444
  84.4 11.7 %copy-start.10 = (f32[5,2,512]{2,1,0:T(2,128)S(1)}, f32[5,2,512]{2,1,0:T(2,128)}, u32[]{:S(2)}) copy-start(f32[5,2,512]{2,1,0:T(2,128)} %get-tuple-element.27) | copy-start | bytes 61444
  84.4 17.3 %collective-permute-start.5 = (f32[128,1,384]{2,0,1:T(8,128)S(1)}, f32[128,1,384]{2,0,1:T(8,128)S(1)}, u32[]{:S(2)}, u32[]{:S(2)}) collective-permute-start(f32[128,1,384]{2,0,1:T(8,128)S(1)} %copy.18), channel_id=1, source_target_pairs={{0,1},{1,0},{2,3},{3,2},{4,5},{5,4},{6,7},{7,6},{8,9},{9,8},{10,11... | collective-permute-start | bytes 589832 | tf_op jit(solution)/shard_map/ppermute | solution.py:312
  87.0 12.3 %collective-permute-start = (f32[5,4,512]{2,1,0:T(4,128)S(1)}, f32[5,4,512]{2,1,0:T(4,128)S(1)}, u32[]{:S(2)}, u32[]{:S(2)}) collective-permute-start(f32[5,4,512]{2,1,0:T(4,128)S(1)} %copy-done.9), channel_id=1, source_target_pairs={{0,32},{32,64},{64,96},{96,128},{128,160},{160,192},{192,224},{224... | collective-permute-start | bytes 122888 | tf_op jit(solution)/shard_map/ppermute | solution.py:300
  87.1 12.2 %collective-permute-start.1 = (f32[5,4,512]{2,1,0:T(4,128)S(1)}, f32[5,4,512]{2,1,0:T(4,128)S(1)}, u32[]{:S(2)}, u32[]{:S(2)}) collective-permute-start(f32[5,4,512]{2,1,0:T(4,128)S(1)} %copy-done.8), channel_id=1, source_target_pairs={{0,224},{32,0},{64,32},{96,64},{128,96},{160,128},{192,160},{224,1... | collective-permute-start | bytes 122888 | tf_op jit(solution)/shard_map/ppermute | solution.py:301
  94.5 1.6 %copy-start.7 = (s32[2,2,4]{2,1,0:T(2,128)S(1)}, s32[2,2,4]{2,1,0:T(2,128)}, u32[]{:S(2)}) copy-start(s32[2,2,4]{2,1,0:T(2,128)} %param.12) | copy-start | bytes 196
  94.5 2.5 %collective-permute-start.2 = (f32[5,2,512]{2,1,0:T(2,128)S(1)}, f32[5,2,512]{2,1,0:T(2,128)S(1)}, u32[]{:S(2)}, u32[]{:S(2)}) collective-permute-start(f32[5,2,512]{2,1,0:T(2,128)S(1)} %copy-done.11), channel_id=1, source_target_pairs={{0,1},{1,2},{2,3},{3,4},{4,5},{5,6},{6,7},{7,8},{8,9},{9,10},{10,1... | collective-permute-start | bytes 61448 | tf_op jit(solution)/shard_map/ppermute | solution.py:302
  96.1 3.2 %collective-permute-start.3 = (f32[5,2,512]{2,1,0:T(2,128)S(1)}, f32[5,2,512]{2,1,0:T(2,128)S(1)}, u32[]{:S(2)}, u32[]{:S(2)}) collective-permute-start(f32[5,2,512]{2,1,0:T(2,128)S(1)} %copy-done.10), channel_id=1, source_target_pairs={{0,31},{1,0},{2,1},{3,2},{4,3},{5,4},{6,5},{7,6},{8,7},{9,8},{10,9... | collective-permute-start | bytes 61448 | tf_op jit(solution)/shard_map/ppermute | solution.py:303
  97.0 2.3 %copy-start.4 = (f32[5,2,512]{2,1,0:T(2,128)}, f32[5,2,512]{2,1,0:T(2,128)S(1)}, u32[]{:S(2)}) copy-start(f32[5,2,512]{2,1,0:T(2,128)S(1)} %collective-permute-done.2.front_ref) | copy-start | bytes 61444
  99.3 0.6 copy-start.5
  99.3 0.6 copy-start.2
  99.3 0.6 copy-start.3
  101.8 0.7 copy-start
  103.9 0.9 slice-start

commit v3 on v2

--- a/solution.py
+++ b/solution.py
@@ -15,7 +15,8 @@
 AXES = ("zhi", "y", "x", "zlo", "core")
 GX = ("zhi", "y")
 GZ = ("x", "zlo", "core")
-CHIPS = ("zhi", "y", "x", "zlo")
+PLANE = ("y", "x")
+COLUMN = ("zhi", "zlo", "core")
 LANES = 128
 NODES = 64
 GROUP = 8
@@ -31,9 +32,17 @@
     return jnp.concatenate([ref[lead + (0,)], ref[lead + (1,)]], axis=0)
 
 
+def squares_kernel(state_ref, out_ref):
+    total = jnp.zeros((2 * state_ref.shape[2], state_ref.shape[3]), F32)
+    for c in range(state_ref.shape[0]):
+        value = rows_of(state_ref, c)
+        total += value * value
+    out_ref[...] = jnp.broadcast_to(jnp.sum(total, keepdims=True), out_ref.shape)
+
+
 def adjoint_kernel(
-    state_ref, cot_ref, inv_ref, w_mid_ref, b_mid_ref,
-    adj_ref, og_ref, xs_ref, w_mid_t_ref, b_col_ref, left_ref, right_ref, front_ref, back_ref,
+    state_ref, cot_ref, inv_ref, w_mid_ref, b_mid_ref, w_out_ref,
+    adj_ref, og_ref, xs_ref, w_mid_t_ref, b_col_ref, w_wide_ref, left_ref, right_ref, front_ref, back_ref,
     rows_ref,
 ):
     channels, _, span, line = state_ref.shape
@@ -88,6 +97,10 @@
         xs_ref[t] = jnp.concatenate([high, tile - high, high, blank], axis=0).astype(BF16)
     w_mid_t_ref[...] = w_mid_ref[...].astype(F32).T.astype(BF16)
     b_col_ref[...] = jnp.broadcast_to(b_mid_ref[...], (LANES, b_mid_ref.shape[1])).T
+    hidden = w_out_ref.shape[0]
+    w_wide_ref[...] = jnp.concatenate(
+        [w_out_ref[...].astype(F32), jnp.zeros((hidden, 2 * GROUP - channels), F32)], axis=1
+    ).astype(BF16)
 
 
 def dot(a, b):
@@ -106,7 +119,7 @@
     entries,
     core_ref, squares_ref, xs_ref, og_ref, w_in_ref, b_in_ref, w_mid_ref, w_mid_t_ref, b_col_ref, w_out_ref,
     back_ref, mine_ref, other_ref,
-    mid_ref, in_ref, out_ref,
+    mid_ref, in_ref, out_ref, wide_ref,
 ):
     cells = xs_ref.shape[0]
     channels, hidden = w_in_ref.shape
@@ -163,16 +176,18 @@
         axis=0,
     )
     half = hidden // 2
-    wide = jnp.concatenate([extra[:, :half], extra[:, half:]], axis=0)
-    wide = jnp.concatenate([wide, jnp.zeros((half - wide.shape[0], half), F32)], axis=0)
+    wide_ref[: 2 * GROUP, :] = extra[:, :half]
+    wide_ref[2 * GROUP :, :] = extra[:, half:]
     core = core_ref[0]
-    own = pl.multiple_of(core * half, half)
-    away = pl.multiple_of((1 - core) * half, half)
-    mine_ref[:, 0, :hidden] = mid_ref[pl.ds(own, half), :]
-    other_ref[:, 0, :hidden] = mid_ref[pl.ds(away, half), :]
-    first_half = core == 0
-    mine_ref[:, 0, hidden:] = jnp.where(first_half, wide, 0.0)
-    other_ref[:, 0, hidden:] = jnp.where(first_half, 0.0, wide)
+    for g in range(hidden // (2 * GROUP)):
+        own = pl.multiple_of(g * 2 * GROUP + core * GROUP, GROUP)
+        away = pl.multiple_of(g * 2 * GROUP + (1 - core) * GROUP, GROUP)
+        for ref, start in ((mine_ref, own), (other_ref, away)):
+            ref[g, :, :hidden] = mid_ref[pl.ds(start, GROUP), :]
+            if g < 2:
+                ref[g, :, hidden:] = wide_ref[pl.ds(start, GROUP), :]
+            else:
+                ref[g, :, hidden:] = jnp.zeros((GROUP, LANES), F32)
 
 
 def finish_kernel(
@@ -187,8 +202,8 @@
     bottom = jnp.zeros((cells, line), F32)
     top = jnp.zeros((cells, line), F32)
     for r in range(cells):
-        bottom = jnp.where(row == r, 1.0 - 2.0 * tags_ref[0, r].astype(F32), bottom)
-        top = jnp.where(row == r, 1.0 - 2.0 * tags_ref[1, r].astype(F32), top)
+        bottom = jnp.where(row == r, 1.0 - 2.0 * tags_ref[0, r // span, r % span].astype(F32), bottom)
+        top = jnp.where(row == r, 1.0 - 2.0 * tags_ref[1, r // span, r % span].astype(F32), top)
     low_wall = lane < NODES
     high_wall = lane >= line - NODES
     for c in range(channels):
@@ -213,11 +228,50 @@
         out_ref[c, 1] = total[span:]
 
 
+def unpack_kernel(sums_ref, in_ref, b_in_ref, mid_ref, b_mid_ref, out_ref):
+    channels, hidden = in_ref.shape
+    mid_ref[...] = sums_ref[:, :hidden]
+    extra = jnp.concatenate(
+        [sums_ref[: 2 * GROUP, hidden:], sums_ref[2 * GROUP : 4 * GROUP, hidden:]], axis=1
+    )
+    in_ref[...] = extra[:channels]
+    b_in_ref[...] = extra[channels : channels + 1]
+    b_mid_ref[...] = extra[GROUP + channels : GROUP + channels + 1]
+    out_ref[...] = extra[GROUP:].T[:, :channels]
+
+
 def shape(*dims, dtype=F32):
     return jax.ShapeDtypeStruct(dims, dtype)
 
 
-def run_adjoint(state, cotangent, local_inverse, w_mid, b_mid):
+def run_squares(state, devices):
+    return pl.pallas_call(
+        squares_kernel,
+        out_shape=shape(devices, LANES),
+        in_specs=whole_vmem(1),
+        out_specs=whole_vmem(1)[0],
+        name="squares",
+    )(state)
+
+
+def run_unpack(sums, channels):
+    hidden = sums.shape[0]
+    return pl.pallas_call(
+        unpack_kernel,
+        out_shape=(
+            shape(channels, hidden),
+            shape(1, hidden),
+            shape(hidden, hidden),
+            shape(1, hidden),
+            shape(hidden, channels),
+        ),
+        in_specs=whole_vmem(1),
+        out_specs=tuple(whole_vmem(5)),
+        name="unpack",
+    )(sums)
+
+
+def run_adjoint(state, cotangent, local_inverse, w_mid, b_mid, w_out):
     channels, _, span, line = state.shape
     cells = 2 * span
     hidden = w_mid.shape[0]
@@ -229,28 +283,28 @@
             shape(cells, 4 * GROUP, line, dtype=BF16),
             shape(hidden, hidden, dtype=BF16),
             shape(hidden, LANES),
+            shape(hidden, 2 * GROUP, dtype=BF16),
             shape(channels, span, line),
             shape(channels, span, line),
             shape(channels, 2, line),
             shape(channels, 2, line),
         ),
-        in_specs=whole_vmem(5),
-        out_specs=tuple(whole_vmem(9)),
+        in_specs=whole_vmem(6),
+        out_specs=tuple(whole_vmem(10)),
         scratch_shapes=[pltpu.VMEM((line // LANES, cells * GROUP, LANES), F32)],
         name="adjoint",
-    )(state, cotangent, local_inverse, w_mid, b_mid.reshape(1, hidden))
+    )(state, cotangent, local_inverse, w_mid, b_mid.reshape(1, hidden), w_out)
 
 
 def run_closure(entries, core, squares, xs, og, w_in, b_in, w_mid, w_mid_t, b_col, w_out):
     cells, _, line = xs.shape
     channels, hidden = w_in.shape
-    half = hidden // 2
     return pl.pallas_call(
         functools.partial(closure_kernel, entries),
         out_shape=(
             shape(line // LANES, cells * GROUP, LANES),
-            shape(half, 1, hidden + LANES),
-            shape(half, 1, hidden + LANES),
+            shape(hidden // (2 * GROUP), GROUP, hidden + LANES),
+            shape(hidden // (2 * GROUP), GROUP, hidden + LANES),
         ),
         in_specs=[pl.BlockSpec(memory_space=pltpu.SMEM)] + whole_vmem(9),
         out_specs=tuple(whole_vmem(3)),
@@ -258,6 +312,7 @@
             pltpu.VMEM((hidden + 2 * GROUP, hidden), F32),
             pltpu.VMEM((2 * GROUP, hidden), F32),
             pltpu.VMEM((2 * GROUP, hidden), F32),
+            pltpu.VMEM((4 * GROUP, LANES), F32),
         ],
         name="closure",
     )(core, squares, xs, og, w_in, b_in.reshape(1, hidden), w_mid, w_mid_t, b_col, w_out)
@@ -286,47 +341,37 @@
     channels, x_elems, z_elems, line = state.shape
     gx, gz = lax.axis_size(GX), lax.axis_size(GZ)
     devices = gx * gz
-    chips = devices // 2
     nodes = x_elems * z_elems * line * devices
-    hidden = w_mid.shape[0]
     swap = [(0, 1), (1, 0)]
     core = lax.axis_index("core")
 
-    squares = jnp.broadcast_to(jnp.sum(state * state), (devices, 1, LANES))
-    squares = exchange(squares, AXES).reshape(devices, LANES)
-    adjoint, og, xs, w_mid_t, b_col, low_x, high_x, low_z, high_z = run_adjoint(
-        state, cotangent, local_inverse, w_mid, b_mid
-    )
-    from_left = lax.ppermute(high_x, GX, ring(gx, 1))
-    from_right = lax.ppermute(low_x, GX, ring(gx, -1))
-    from_front = lax.ppermute(high_z, GZ, ring(gz, 1))
-    from_rear = lax.ppermute(low_z, GZ, ring(gz, -1))
-    w_out_wide = jnp.pad(w_out, ((0, 0), (0, 2 * GROUP - channels)))
+    squares = exchange(run_squares(state, devices).reshape(devices, 1, LANES), AXES)
+    adjoint, og, xs, w_mid_t, b_col, w_wide, low_x, high_x, low_z, high_z = run_adjoint(
+        state, cotangent, local_inverse, w_mid, b_mid, w_out
+    )
+    halo = (
+        lax.ppermute(high_x, GX, ring(gx, 1)),
+        lax.ppermute(low_x, GX, ring(gx, -1)),
+        lax.ppermute(high_z, GZ, ring(gz, 1)),
+        lax.ppermute(low_z, GZ, ring(gz, -1)),
+    )
+    squares, halo = lax.optimization_barrier((squares, halo))
     back, mine, other = run_closure(
-        float(channels * nodes), core.reshape(1), squares, xs, og, w_in, b_in, w_mid, w_mid_t, b_col, w_out_wide
-    )
+        float(channels * nodes), core.reshape(1), squares.reshape(devices, LANES), xs, og, w_in, b_in, w_mid,
+        w_mid_t, b_col, w_wide,
+    )
+    grad_state = run_finish(wall_tags, adjoint, back, *halo)
     mine = mine + lax.ppermute(other, "core", swap)
     factor = 4.0 / math.sqrt(nodes)
-    chunk = factor * jnp.sum(exchange(mine, CHIPS), axis=0, keepdims=True)
-    gathered = exchange(jnp.broadcast_to(chunk, (chips,) + chunk.shape[1:]), CHIPS)
-    partner = lax.ppermute(gathered, "core", swap)
-    grad_state = run_finish(
-        wall_tags.reshape(2, x_elems * z_elems), adjoint, back, from_left, from_right, from_front, from_rear
-    )
-    gathered, partner = gathered[:, 0], partner[:, 0]
-    first = jnp.where(core == 0, gathered, partner)
-    second = jnp.where(core == 0, partner, gathered)
-    grad_mid = jnp.concatenate([first[:, :hidden], second[:, :hidden]], axis=0)
-    extra = jnp.concatenate([first[: 2 * GROUP, hidden:], first[2 * GROUP : 4 * GROUP, hidden:]], axis=1)
-    c = channels
-    return (
-        grad_state,
-        extra[:c],
-        extra[c],
-        grad_mid,
-        extra[GROUP + c],
-        extra[GROUP : GROUP + c].T,
-    )
+    part = jnp.sum(exchange(mine, PLANE), axis=0)
+    part = exchange(jnp.broadcast_to(part, (lax.axis_size(COLUMN),) + part.shape), COLUMN)
+    part = factor * jnp.sum(part.reshape(-1, 2, *part.shape[1:]), axis=0)
+    part = part.reshape(-1, part.shape[-1])
+    sums = exchange(jnp.broadcast_to(part, (lax.axis_size(PLANE),) + part.shape), PLANE)
+    grad_in, grad_b_in, grad_mid, grad_b_mid, grad_out = run_unpack(
+        sums.reshape(-1, sums.shape[-1]), channels
+    )
+    return grad_state, grad_in, grad_b_in[0], grad_mid, grad_b_mid[0], grad_out
 
 
 def solution(mesh):

time: 107 us -> 103 us (0.963)
  blocking collectives: 38.1 us -> 29 us
  starting transfers between devices: 28.3 us -> 33.9 us
  other arithmetic: 5.02 us -> 0.99 us
  Pallas kernels: 16.9 us -> 20.4 us
  waiting for transfers between devices: 10.1 us -> 12.9 us
  local copies, waits for them, and re-layouts: 6.43 us -> 4.54 us
    all_to_all x2, blocking collectives: 38.1 us -> 29 us  [exchange(): return lax.all_to_all(value, axes, 0, 0, tiled=True)]
    all_to_all x1 -> x2, starting transfers between devices: 15.6 us -> 19.2 us  [exchange(): return lax.all_to_all(value, axes, 0, 0, tiled=True)]
    pallas_call x0 -> x2, Pallas kernels: none -> 3.45 us  [the longest x1 1.78 us: run_unpack(): pl.pallas_call(unpack_kernel, out_shape=(shape(channels, hidden), shape(1...]
    ppermute x1, starting transfers between devices: 0.99 us -> 4.41 us  [per_device(): mine = mine + lax.ppermute(other, 'core', swap)]
    all_to_all x1 -> x2, waiting for transfers between devices: 6.24 us -> 8.57 us  [exchange(): return lax.all_to_all(value, axes, 0, 0, tiled=True)]
    reduce_sum x2, other arithmetic: 1.71 us -> 0.04 us  [the longest x1 0.02 us: per_device(): part = jnp.sum(exchange(mine, PLANE), axis=0)]
    ppermute x5 -> x4, starting transfers between devices: 11.7 us -> 10.3 us  [the longest x1 7.24 us: per_device(): lax.ppermute(low_x, GX, ring(gx, -1))]
    concatenate x2 -> x0, other arithmetic: 1.29 us -> none  [the longest x1 0.72 us: per_device(): grad_mid = jnp.concatenate([first[:, :hidden], second[:, :hidden]], axis=0)]
where the time goes in v3:
time: 103 us; the launch traced here: 102 us
  starting transfers between devices  33.9 us (33%)
  blocking collectives  29 us (28%)
  Pallas kernels  20.4 us (20%)
  waiting for transfers between devices  12.9 us (13%)
  local copies, waits for them, and re-layouts  4.54 us (4%)
    all_to_all x2, blocking collectives, exchange(): return lax.all_to_all(value, axes, 0, 0, tiled=True)  29 us
    all_to_all x2, starting transfers between devices, exchange(): return lax.all_to_all(value, axes, 0, 0, tiled=True)  19.2 us
    pallas_call x1, Pallas kernels, run_closure(): pl.pallas_call(functools.partial(closure_kernel, entries), out_shape=(sha...  9.98 us
    all_to_all x2, waiting for transfers between devices, exchange(): return lax.all_to_all(value, axes, 0, 0, tiled=True)  8.57 us
    ppermute x1, starting transfers between devices, per_device(): lax.ppermute(low_x, GX, ring(gx, -1))  7.24 us
    pallas_call x1, Pallas kernels, run_adjoint(): pl.pallas_call(adjoint_kernel, out_shape=(shape(channels, cells, line), s...  5.08 us
    ppermute x1, starting transfers between devices, per_device(): mine = mine + lax.ppermute(other, 'core', swap)  4.41 us
    unnamed x16, local copies, waits for them, and re-layouts  3.76 us
  transfers between devices with their start and end apart: 7, of which 4 were waited for; matrix products, arithmetic and copies ran while one was open for 1% of the time, Pallas kernels for 7%

profile of v3, /device:TPU:1, one launch (start us, length us, event | category | flops | bytes accessed | tf_op | source)
XLA Modules:
  0.0 102.4 jit_solution(5372000323770739861)
XLA Ops:
  0.6 1.7 %squares.1 = f32[256,128]{1,0:T(8,128)} custom-call(f32[5,2,4,512]{3,2,1,0:T(4,128)} %state_ref.3), custom_call_target="tpu_custom_call" | custom-call | tf_op jit(solution)/shard_map/squares/pallas_call | solution.py:248
  2.3 0.0 copy-start.6
  2.3 15.6 %all-to-all-start = ((f32[256,1,128]{2,1,0:T(1,128)}), f32[256,1,128]{2,1,0:T(1,128)S(1)}, u32[]{:S(2)}, u32[]{:S(2)}) async-start(f32[256,1,128]{2,1,0:T(1,128)} %bitcast.16), calls=%async_computation | async-start | bytes 262144 | tf_op jit(solution)/shard_map/all_to_all | solution.py:337
  18.0 0.0 copy-done.6
  18.0 0.8 copy.20.w_out_ref
  18.7 5.1 %adjoint.1 = (f32[5,8,512]{2,1,0:T(8,128)}, bf16[8,16,512]{2,1,0:T(8,128)(2,1)}, bf16[8,32,512]{2,1,0:T(8,128)(2,1)}, bf16[256,256]{1,0:T(8,128)(2,1)}, f32[256,...) custom-call(f32[5,2,4,512]{3,2,1,0:T(4,128)} %state_ref.3, ...), custom_call_target="tpu_custom_call" | custom-call | tf_op jit(solution)/shard_map/adjoint/pallas_call | solution.py:278
  23.8 1.4 %collective-permute-start = (f32[5,4,512]{2,1,0:T(4,128)}, f32[5,4,512]{2,1,0:T(4,128)S(1)}, u32[]{:S(2)}, u32[]{:S(2)}) collective-permute-start(f32[5,4,512]{2,1,0:T(4,128)} %get-tuple-element.30), channel_id=1, source_target_pairs={{0,32},{32,64},{64,96},{96,128},{128,160},{160,192},{192,224},{224... | collective-permute-start | bytes 122888 | tf_op jit(solution)/shard_map/ppermute | solution.py:353
  25.2 7.2 %collective-permute-start.1 = (f32[5,4,512]{2,1,0:T(4,128)}, f32[5,4,512]{2,1,0:T(4,128)S(1)}, u32[]{:S(2)}, u32[]{:S(2)}) collective-permute-start(f32[5,4,512]{2,1,0:T(4,128)} %get-tuple-element.31), channel_id=1, source_target_pairs={{0,224},{32,0},{64,32},{96,64},{128,96},{160,128},{192,160},{224,1... | collective-permute-start | bytes 122888 | tf_op jit(solution)/shard_map/ppermute | solution.py:354
  32.5 1.2 %collective-permute-start.2 = (f32[5,2,512]{2,1,0:T(2,128)}, f32[5,2,512]{2,1,0:T(2,128)S(1)}, u32[]{:S(2)}, u32[]{:S(2)}) collective-permute-start(f32[5,2,512]{2,1,0:T(2,128)} %get-tuple-element.32), channel_id=1, source_target_pairs={{0,1},{1,2},{2,3},{3,4},{4,5},{5,6},{6,7},{7,8},{8,9},{9,10},{10,1... | collective-permute-start | bytes 61448 | tf_op jit(solution)/shard_map/ppermute | solution.py:355
  33.7 0.4 collective-permute-start.3
  34.1 0.9 collective-permute-done.2.front_ref
  35.0 0.0 copy-start.4
  35.0 2.1 %collective-permute-done.3.rear_ref = f32[5,2,512]{2,1,0:T(2,128)S(1)} collective-permute-done((f32[5,2,512]{2,1,0:T(2,128)}, f32[5,2,512]{2,1,0:T(2,128)S(1)}, u32[]{:S(2)}, u32[]{:S(2)}) %collective-permute-start.3) | collective-permute-done | bytes 20512 | tf_op jit(solution)/shard_map/ppermute | solution.py:356
  37.1 0.0 copy-start.5
  37.1 0.0 collective-permute-done.left_ref
  37.1 0.0 copy-start.2
  37.1 0.0 collective-permute-done.1.right_ref
  37.1 0.0 copy-start.3
  37.1 0.0 all-to-all-done
  37.1 0.0 copy-start.1
  37.1 0.7 copy-done.1
  37.8 10.0 %closure.1 = (f32[4,64,128]{2,1,0:T(8,128)}, f32[16,8,384]{2,1,0:T(8,128)}, f32[16,8,384]{2,1,0:T(8,128)}) custom-call(s32[1]{0:T(128)} %bitcast.1.core_ref, f32[256,128]{1,0:T(8,128)} %bitcast.15, bf16[8,32,512]{2,1,0:T(8,128)(2,1)} %get-tuple-element.35.xs_ref, bf16[8,16,512]{2,1,0:T(8,128)(2,1)} %get-tuple-element.36.og_ref, f32[5,256]{1,0:T(8,128)} %w_in_ref.1, ...), custom_call_target="tpu_custom_call" | custom-call | tf_op jit(solution)/shard_map/closure/pallas_call | solution.py:302
  47.8 0.0 copy-done.4
  47.8 0.0 copy-done.5
  47.8 0.0 copy-done.2
  47.8 0.0 copy-done.3
  47.8 4.4 %collective-permute-start.4 = (f32[16,8,384]{2,1,0:T(8,128)}, f32[16,8,384]{2,1,0:T(8,128)S(1)}, u32[]{:S(2)}, u32[]{:S(2)}) collective-permute-start(f32[16,8,384]{2,1,0:T(8,128)} %get-tuple-element.46), channel_id=1, source_target_pairs={{0,1},{1,0},{2,3},{3,2},{4,5},{5,4},{6,7},{7,6},{8,9},{9,8},{10,11... | collective-permute-start | bytes 589832 | tf_op jit(solution)/shard_map/ppermute | solution.py:364
  52.2 1.3 %collective-permute-done.4 = f32[16,8,384]{2,1,0:T(8,128)S(1)} collective-permute-done((f32[16,8,384]{2,1,0:T(8,128)}, f32[16,8,384]{2,1,0:T(8,128)S(1)}, u32[]{:S(2)}, u32[]{:S(2)}) %collective-permute-start.4) | collective-permute-done | bytes 196640 | tf_op jit(solution)/shard_map/ppermute | solution.py:364
  53.5 0.9 add.3
  54.5 13.0 %all_to_all.20 = f32[16,8,384]{2,1,0:T(8,128)S(1)} all-to-all(f32[16,8,384]{2,1,0:T(8,128)S(1)} %add.3), channel_id=1, replica_groups=mesh['zhi'=2,'y'=4,'x'=4,'zlo'=4,'core'=2] {'y','x'}, dimensions={0} | all-to-all | bytes 393216 | tf_op jit(solution)/shard_map/all_to_all | solution.py:337
  67.5 16.1 %all_to_all.21 = f32[16,8,384]{2,1,0:T(8,128)S(1)} all-to-all(f32[16,8,384]{2,1,0:T(8,128)S(1)} %broadcast_in_dim.6), channel_id=1, replica_groups=mesh['zhi'=2,'y'=4,'x'=4,'zlo'=4,'core'=2] {'zhi','zlo','core'}, dimensions={0} | all-to-all | bytes 393216 | tf_op jit(solution)/shard_map/all_to_all | solution.py:337
  83.6 0.8 broadcast_in_dim.7
  84.3 3.6 %all-to-all-start.3 = ((f32[16,16,384]{2,1,0:T(8,128)}), f32[16,16,384]{2,1,0:T(8,128)S(1)}, u32[]{:S(2)}, u32[]{:S(2)}) async-start(f32[16,16,384]{2,1,0:T(8,128)} %broadcast_in_dim.7), calls=%async_computation.3 | async-start | bytes 786432 | tf_op jit(solution)/shard_map/all_to_all | solution.py:337
  87.9 1.8 %finish.1 = f32[5,2,4,512]{3,2,1,0:T(4,128)} custom-call(s32[2,2,4]{2,1,0:T(2,128)} %tags_ref.1, f32[5,8,512]{2,1,0:T(8,128)} %get-tuple-element.29.adj_ref, f32[4,64,128]{2,1,0:T(8,128)} %get-tuple-element.40.back_ref, f32[5,4,512]{2,1,0:T(4,128)} %copy-done.2, f32[5,4,512]{2,1,0:T(4,128)} %copy-done.3, f32[5,2,512]{2,1,0:T(2,128)} %copy-done.4, ...), custom_call_target="tpu_custom_call" | custom-call | tf_op jit(solution)/shard_map/finish/pallas_call | solution.py:323
  89.7 8.6 %all-to-all-done.3 = f32[16,16,384]{2,1,0:T(8,128)S(1)} async-done(((f32[16,16,384]{2,1,0:T(8,128)}), f32[16,16,384]{2,1,0:T(8,128)S(1)}, u32[]{:S(2)}, u32[]{:S(2)}) %all-to-all-start.3) | async-done | bytes 393248 | tf_op jit(solution)/shard_map/all_to_all | solution.py:337
  98.3 0.0 copy-start
  98.3 0.7 copy-done
  99.1 1.8 %unpack.1 = (f32[5,256]{1,0:T(8,128)}, f32[1,256]{1,0:T(1,128)}, f32[256,256]{1,0:T(8,128)}, f32[1,256]{1,0:T(1,128)}, f32[256,5]{1,0:T(8,128)}) custom-call(f32[256,384]{1,0:T(8,128)} %bitcast.13), custom_call_target="tpu_custom_call" | custom-call | tf_op jit(solution)/shard_map/unpack/pallas_call | solution.py:259
  100.8 1.6 %copy.22 = f32[256,5]{0,1:T(8,128)} copy(f32[256,5]{1,0:T(8,128)} %get-tuple-element.69) | data formatting | bytes 10240
  (4 shorter events, 0.1 us)
Async XLA Ops:
  2.3 15.7 %copy-start.6 = (bf16[256,5]{0,1:T(8,128)(2,1)S(1)}, bf16[256,5]{0,1:T(8,128)(2,1)}, u32[]{:S(2)}) copy-start(bf16[256,5]{0,1:T(8,128)(2,1)} %param.17) | copy-start | bytes 7684
  2.3 34.8 %all-to-all-start = ((f32[256,1,128]{2,1,0:T(1,128)}), f32[256,1,128]{2,1,0:T(1,128)S(1)}, u32[]{:S(2)}, u32[]{:S(2)}) async-start(f32[256,1,128]{2,1,0:T(1,128)} %bitcast.16), calls=%async_computation | async-start | bytes 262144 | tf_op jit(solution)/shard_map/all_to_all | solution.py:337
  23.8 13.3 %collective-permute-start = (f32[5,4,512]{2,1,0:T(4,128)}, f32[5,4,512]{2,1,0:T(4,128)S(1)}, u32[]{:S(2)}, u32[]{:S(2)}) collective-permute-start(f32[5,4,512]{2,1,0:T(4,128)} %get-tuple-element.30), channel_id=1, source_target_pairs={{0,32},{32,64},{64,96},{96,128},{128,160},{160,192},{192,224},{224... | collective-permute-start | bytes 122888 | tf_op jit(solution)/shard_map/ppermute | solution.py:353
  25.2 11.9 %collective-permute-start.1 = (f32[5,4,512]{2,1,0:T(4,128)}, f32[5,4,512]{2,1,0:T(4,128)S(1)}, u32[]{:S(2)}, u32[]{:S(2)}) collective-permute-start(f32[5,4,512]{2,1,0:T(4,128)} %get-tuple-element.31), channel_id=1, source_target_pairs={{0,224},{32,0},{64,32},{96,64},{128,96},{160,128},{192,160},{224,1... | collective-permute-start | bytes 122888 | tf_op jit(solution)/shard_map/ppermute | solution.py:354
  32.5 2.5 %collective-permute-start.2 = (f32[5,2,512]{2,1,0:T(2,128)}, f32[5,2,512]{2,1,0:T(2,128)S(1)}, u32[]{:S(2)}, u32[]{:S(2)}) collective-permute-start(f32[5,2,512]{2,1,0:T(2,128)} %get-tuple-element.32), channel_id=1, source_target_pairs={{0,1},{1,2},{2,3},{3,4},{4,5},{5,6},{6,7},{7,8},{8,9},{9,10},{10,1... | collective-permute-start | bytes 61448 | tf_op jit(solution)/shard_map/ppermute | solution.py:355
  33.7 3.4 %collective-permute-start.3 = (f32[5,2,512]{2,1,0:T(2,128)}, f32[5,2,512]{2,1,0:T(2,128)S(1)}, u32[]{:S(2)}, u32[]{:S(2)}) collective-permute-start(f32[5,2,512]{2,1,0:T(2,128)} %get-tuple-element.33), channel_id=1, source_target_pairs={{0,31},{1,0},{2,1},{3,2},{4,3},{5,4},{6,5},{7,6},{8,7},{9,8},{10,9... | collective-permute-start | bytes 61448 | tf_op jit(solution)/shard_map/ppermute | solution.py:356
  35.0 12.8 %copy-start.4 = (f32[5,2,512]{2,1,0:T(2,128)}, f32[5,2,512]{2,1,0:T(2,128)S(1)}, u32[]{:S(2)}) copy-start(f32[5,2,512]{2,1,0:T(2,128)S(1)} %collective-permute-done.2.front_ref) | copy-start | bytes 61444
  37.1 10.7 %copy-start.5 = (f32[5,2,512]{2,1,0:T(2,128)}, f32[5,2,512]{2,1,0:T(2,128)S(1)}, u32[]{:S(2)}) copy-start(f32[5,2,512]{2,1,0:T(2,128)S(1)} %collective-permute-done.3.rear_ref) | copy-start | bytes 61444
  37.1 10.7 %copy-start.2 = (f32[5,4,512]{2,1,0:T(4,128)}, f32[5,4,512]{2,1,0:T(4,128)S(1)}, u32[]{:S(2)}) copy-start(f32[5,4,512]{2,1,0:T(4,128)S(1)} %collective-permute-done.left_ref) | copy-start | bytes 122884
  37.1 10.7 %copy-start.3 = (f32[5,4,512]{2,1,0:T(4,128)}, f32[5,4,512]{2,1,0:T(4,128)S(1)}, u32[]{:S(2)}) copy-start(f32[5,4,512]{2,1,0:T(4,128)S(1)} %collective-permute-done.1.right_ref) | copy-start | bytes 122884
  37.1 0.7 copy-start.1
  47.8 5.7 %collective-permute-start.4 = (f32[16,8,384]{2,1,0:T(8,128)}, f32[16,8,384]{2,1,0:T(8,128)S(1)}, u32[]{:S(2)}, u32[]{:S(2)}) collective-permute-start(f32[16,8,384]{2,1,0:T(8,128)} %get-tuple-element.46), channel_id=1, source_target_pairs={{0,1},{1,0},{2,3},{3,2},{4,5},{5,4},{6,7},{7,6},{8,9},{9,8},{10,11... | collective-permute-start | bytes 589832 | tf_op jit(solution)/shard_map/ppermute | solution.py:364
  84.3 14.0 %all-to-all-start.3 = ((f32[16,16,384]{2,1,0:T(8,128)}), f32[16,16,384]{2,1,0:T(8,128)S(1)}, u32[]{:S(2)}, u32[]{:S(2)}) async-start(f32[16,16,384]{2,1,0:T(8,128)} %broadcast_in_dim.7), calls=%async_computation.3 | async-start | bytes 786432 | tf_op jit(solution)/shard_map/all_to_all | solution.py:337
  98.3 0.7 copy-start

commit v4 on v3

--- a/solution.py
+++ b/solution.py
@@ -8,6 +8,7 @@
 from jax.experimental.pallas import tpu as pltpu
 from jax.sharding import Mesh, PartitionSpec as P
 
+
 KAPPA = 0.5
 DT_STEP = 0.5
 EPS = 1e-06
@@ -17,6 +18,7 @@
 GZ = ("x", "zlo", "core")
 PLANE = ("y", "x")
 COLUMN = ("zhi", "zlo", "core")
+TOWER = ("zhi", "zlo")
 LANES = 128
 NODES = 64
 GROUP = 8
@@ -97,10 +99,10 @@
         xs_ref[t] = jnp.concatenate([high, tile - high, high, blank], axis=0).astype(BF16)
     w_mid_t_ref[...] = w_mid_ref[...].astype(F32).T.astype(BF16)
     b_col_ref[...] = jnp.broadcast_to(b_mid_ref[...], (LANES, b_mid_ref.shape[1])).T
-    hidden = w_out_ref.shape[0]
+    hidden = w_out_ref.shape[1]
     w_wide_ref[...] = jnp.concatenate(
-        [w_out_ref[...].astype(F32), jnp.zeros((hidden, 2 * GROUP - channels), F32)], axis=1
-    ).astype(BF16)
+        [w_out_ref[...].astype(F32), jnp.zeros((2 * GROUP - channels, hidden), F32)], axis=0
+    ).T.astype(BF16)
 
 
 def dot(a, b):
@@ -176,18 +178,14 @@
         axis=0,
     )
     half = hidden // 2
-    wide_ref[: 2 * GROUP, :] = extra[:, :half]
-    wide_ref[2 * GROUP :, :] = extra[:, half:]
+    wide_ref[0] = extra[:, :half]
+    wide_ref[1] = extra[:, half:]
     core = core_ref[0]
-    for g in range(hidden // (2 * GROUP)):
-        own = pl.multiple_of(g * 2 * GROUP + core * GROUP, GROUP)
-        away = pl.multiple_of(g * 2 * GROUP + (1 - core) * GROUP, GROUP)
-        for ref, start in ((mine_ref, own), (other_ref, away)):
-            ref[g, :, :hidden] = mid_ref[pl.ds(start, GROUP), :]
-            if g < 2:
-                ref[g, :, hidden:] = wide_ref[pl.ds(start, GROUP), :]
-            else:
-                ref[g, :, hidden:] = jnp.zeros((GROUP, LANES), F32)
+    for ref, place in ((mine_ref, core), (other_ref, 1 - core)):
+        start = pl.multiple_of(place * half, half)
+        ref[:half, :] = mid_ref[pl.ds(start, half), :half]
+        ref[half:hidden, :] = mid_ref[pl.ds(start, half), half:]
+        ref[hidden:, :] = wide_ref[place]
 
 
 def finish_kernel(
@@ -228,34 +226,38 @@
         out_ref[c, 1] = total[span:]
 
 
-def unpack_kernel(sums_ref, in_ref, b_in_ref, mid_ref, b_mid_ref, out_ref):
+def unpack_kernel(core_ref, own_ref, away_ref, in_ref, b_in_ref, mid_ref, b_mid_ref, out_ref):
     channels, hidden = in_ref.shape
-    mid_ref[...] = sums_ref[:, :hidden]
-    extra = jnp.concatenate(
-        [sums_ref[: 2 * GROUP, hidden:], sums_ref[2 * GROUP : 4 * GROUP, hidden:]], axis=1
-    )
+    half = hidden // 2
+    own, away = own_ref[...], away_ref[...]
+    first = jnp.where(core_ref[0] == 0, own, away)
+    second = jnp.where(core_ref[0] == 0, away, own)
+    for k, part in enumerate((first, second)):
+        mid_ref[k * half : (k + 1) * half, :half] = part[:half]
+        mid_ref[k * half : (k + 1) * half, half:] = part[half:hidden]
+    extra = jnp.concatenate([first[hidden:], second[hidden:]], axis=1)
     in_ref[...] = extra[:channels]
     b_in_ref[...] = extra[channels : channels + 1]
+    out_ref[...] = extra[GROUP : GROUP + channels]
     b_mid_ref[...] = extra[GROUP + channels : GROUP + channels + 1]
-    out_ref[...] = extra[GROUP:].T[:, :channels]
 
 
 def shape(*dims, dtype=F32):
     return jax.ShapeDtypeStruct(dims, dtype)
 
 
-def run_squares(state, devices):
+def run_squares(state, peers):
     return pl.pallas_call(
         squares_kernel,
-        out_shape=shape(devices, LANES),
+        out_shape=shape(peers, LANES),
         in_specs=whole_vmem(1),
         out_specs=whole_vmem(1)[0],
         name="squares",
     )(state)
 
 
-def run_unpack(sums, channels):
-    hidden = sums.shape[0]
+def run_unpack(core, own, away, channels):
+    hidden = own.shape[0] - 2 * GROUP
     return pl.pallas_call(
         unpack_kernel,
         out_shape=(
@@ -263,12 +265,12 @@
             shape(1, hidden),
             shape(hidden, hidden),
             shape(1, hidden),
-            shape(hidden, channels),
+            shape(channels, hidden),
         ),
-        in_specs=whole_vmem(1),
+        in_specs=[pl.BlockSpec(memory_space=pltpu.SMEM)] + whole_vmem(2),
         out_specs=tuple(whole_vmem(5)),
         name="unpack",
-    )(sums)
+    )(core, own, away)
 
 
 def run_adjoint(state, cotangent, local_inverse, w_mid, b_mid, w_out):
@@ -293,18 +295,18 @@
         out_specs=tuple(whole_vmem(10)),
         scratch_shapes=[pltpu.VMEM((line // LANES, cells * GROUP, LANES), F32)],
         name="adjoint",
-    )(state, cotangent, local_inverse, w_mid, b_mid.reshape(1, hidden), w_out)
+    )(state, cotangent, local_inverse, w_mid, b_mid.reshape(1, hidden), w_out.T)
 
 
 def run_closure(entries, core, squares, xs, og, w_in, b_in, w_mid, w_mid_t, b_col, w_out):
     cells, _, line = xs.shape
-    channels, hidden = w_in.shape
+    _, hidden = w_in.shape
     return pl.pallas_call(
         functools.partial(closure_kernel, entries),
         out_shape=(
             shape(line // LANES, cells * GROUP, LANES),
-            shape(hidden // (2 * GROUP), GROUP, hidden + LANES),
-            shape(hidden // (2 * GROUP), GROUP, hidden + LANES),
+            shape(hidden + 2 * GROUP, LANES),
+            shape(hidden + 2 * GROUP, LANES),
         ),
         in_specs=[pl.BlockSpec(memory_space=pltpu.SMEM)] + whole_vmem(9),
         out_specs=tuple(whole_vmem(3)),
@@ -312,7 +314,7 @@
             pltpu.VMEM((hidden + 2 * GROUP, hidden), F32),
             pltpu.VMEM((2 * GROUP, hidden), F32),
             pltpu.VMEM((2 * GROUP, hidden), F32),
-            pltpu.VMEM((4 * GROUP, LANES), F32),
+            pltpu.VMEM((2, 2 * GROUP, LANES), F32),
         ],
         name="closure",
     )(core, squares, xs, og, w_in, b_in.reshape(1, hidden), w_mid, w_mid_t, b_col, w_out)
@@ -345,33 +347,35 @@
     swap = [(0, 1), (1, 0)]
     core = lax.axis_index("core")
 
-    squares = exchange(run_squares(state, devices).reshape(devices, 1, LANES), AXES)
+    plane, column, tower = lax.axis_size(PLANE), lax.axis_size(COLUMN), lax.axis_size(TOWER)
+    squares = run_squares(state, plane).reshape(plane, 1, LANES)
+    squares = exchange(squares, PLANE)
+    squares = jnp.broadcast_to(jnp.sum(squares, axis=0, keepdims=True), (column, 1, LANES))
+    squares = exchange(squares, COLUMN)
     adjoint, og, xs, w_mid_t, b_col, w_wide, low_x, high_x, low_z, high_z = run_adjoint(
         state, cotangent, local_inverse, w_mid, b_mid, w_out
     )
-    halo = (
-        lax.ppermute(high_x, GX, ring(gx, 1)),
-        lax.ppermute(low_x, GX, ring(gx, -1)),
-        lax.ppermute(high_z, GZ, ring(gz, 1)),
-        lax.ppermute(low_z, GZ, ring(gz, -1)),
-    )
-    squares, halo = lax.optimization_barrier((squares, halo))
+    sends = ((high_x, GX, gx, 1), (low_x, GX, gx, -1), (high_z, GZ, gz, 1), (low_z, GZ, gz, -1))
+    halo = []
+    for face, axes, count, way in sends:
+        halo.append(lax.ppermute(face, axes, ring(count, way)))
+    core = core.reshape(1)
     back, mine, other = run_closure(
-        float(channels * nodes), core.reshape(1), squares.reshape(devices, LANES), xs, og, w_in, b_in, w_mid,
+        float(channels * nodes), core, squares.reshape(column, LANES), xs, og, w_in, b_in, w_mid,
         w_mid_t, b_col, w_wide,
     )
     grad_state = run_finish(wall_tags, adjoint, back, *halo)
     mine = mine + lax.ppermute(other, "core", swap)
     factor = 4.0 / math.sqrt(nodes)
-    part = jnp.sum(exchange(mine, PLANE), axis=0)
-    part = exchange(jnp.broadcast_to(part, (lax.axis_size(COLUMN),) + part.shape), COLUMN)
-    part = factor * jnp.sum(part.reshape(-1, 2, *part.shape[1:]), axis=0)
-    part = part.reshape(-1, part.shape[-1])
-    sums = exchange(jnp.broadcast_to(part, (lax.axis_size(PLANE),) + part.shape), PLANE)
-    grad_in, grad_b_in, grad_mid, grad_b_mid, grad_out = run_unpack(
-        sums.reshape(-1, sums.shape[-1]), channels
-    )
-    return grad_state, grad_in, grad_b_in[0], grad_mid, grad_b_mid[0], grad_out
+    width = mine.shape[0] // plane
+    part = exchange(mine.reshape(plane, width, 1, LANES), PLANE)
+    part = jnp.broadcast_to(jnp.sum(part, axis=0, keepdims=True), (tower, width, 1, LANES))
+    part = exchange(part, TOWER)
+    part = jnp.broadcast_to(factor * jnp.sum(part, axis=0, keepdims=True), (plane, width, 1, LANES))
+    own = exchange(part, PLANE).reshape(mine.shape)
+    away = lax.ppermute(own, "core", swap)
+    grad_in, grad_b_in, grad_mid, grad_b_mid, grad_out = run_unpack(core, own, away, channels)
+    return grad_state, grad_in, grad_b_in[0], grad_mid, grad_b_mid[0], grad_out.T
 
 
 def solution(mesh):

time: 103 us -> 102 us (level)
  the two profiles are of different devices: /device:TPU:1 before, /device:TPU:103 now
where the time goes in v4:
time: 102 us
  blocking collectives  41.5 us (41%)
  starting transfers between devices  27.1 us (27%)
  Pallas kernels  20.2 us (20%)
  waiting for transfers between devices  8.33 us (8%)
  local copies, waits for them, and re-layouts  2.57 us (3%)
  other arithmetic  1.11 us (1%)
    all_to_all x4, blocking collectives, exchange(): return lax.all_to_all(value, axes, 0, 0, tiled=True)  41.5 us
    ppermute x4, starting transfers between devices, per_device(): halo.append(lax.ppermute(face, axes, ring(count, way)))  12.9 us
    pallas_call x1, Pallas kernels, run_closure(): pl.pallas_call(functools.partial(closure_kernel, entries), out_shape=(sha...  9.88 us
    all_to_all x1, starting transfers between devices, exchange(): return lax.all_to_all(value, axes, 0, 0, tiled=True)  9.39 us
    ppermute x4, waiting for transfers between devices, per_device(): halo.append(lax.ppermute(face, axes, ring(count, way)))  7.11 us
    pallas_call x1, Pallas kernels, run_adjoint(): pl.pallas_call(adjoint_kernel, out_shape=(shape(channels, cells, line), s...  5.15 us
    ppermute x1, starting transfers between devices, per_device(): away = lax.ppermute(own, 'core', swap)  4.36 us
  transfers between devices with their start and end apart: 7, of which 3 were waited for; matrix products, arithmetic and copies ran while one was open for 0% of the time, Pallas kernels for 7%

profile of v4, /device:TPU:103, one launch (start us, length us, event | category | flops | bytes accessed | tf_op | source)
XLA Modules:
  0.0 101.5 jit_solution(16917705767391235727)
XLA Ops:
  0.6 1.6 %squares.1 = f32[16,128]{1,0:T(8,128)} custom-call(f32[5,2,4,512]{3,2,1,0:T(4,128)} %state_ref.3), custom_call_target="tpu_custom_call" | custom-call | tf_op jit(solution)/shard_map/squares/pallas_call | solution.py:250
  2.2 11.5 %all_to_all.25 = f32[16,1,128]{2,1,0:T(1,128)S(1)} all-to-all(f32[16,1,128]{2,1,0:T(1,128)} %bitcast.17), channel_id=1, replica_groups=mesh['zhi'=2,'y'=4,'x'=4,'zlo'=4,'core'=2] {'y','x'}, dimensions={0} | all-to-all | bytes 16384 | tf_op jit(solution)/shard_map/all_to_all | solution.py:339
  13.8 0.6 broadcast_in_dim.6
  14.4 9.4 %all-to-all-start.1 = ((f32[16,1,128]{2,1,0:T(1,128)}), f32[16,1,128]{2,1,0:T(1,128)S(1)}, u32[]{:S(2)}, u32[]{:S(2)}) async-start(f32[16,1,128]{2,1,0:T(1,128)} %broadcast_in_dim.6), calls=%async_computation.1 | async-start | bytes 16384 | tf_op jit(solution)/shard_map/all_to_all | solution.py:339
  23.8 5.1 %adjoint.1 = (f32[5,8,512]{2,1,0:T(8,128)}, bf16[8,16,512]{2,1,0:T(8,128)(2,1)}, bf16[8,32,512]{2,1,0:T(8,128)(2,1)}, bf16[256,256]{1,0:T(8,128)(2,1)}, f32[256,...) custom-call(f32[5,2,4,512]{3,2,1,0:T(4,128)} %state_ref.3, ...), custom_call_target="tpu_custom_call" | custom-call | tf_op jit(solution)/shard_map/adjoint/pallas_call | solution.py:280
  29.0 0.0 all-to-all-done.1
  29.0 0.0 copy-start.4
  29.0 0.6 copy-done.4
  29.6 9.9 %closure.1 = (f32[4,64,128]{2,1,0:T(8,128)}, f32[272,128]{1,0:T(8,128)}, f32[272,128]{1,0:T(8,128)}) custom-call(s32[1]{0:T(128)} %bitcast.2.core_ref, f32[16,128]{1,0:T(8,128)} %bitcast.16, bf16[8,32,512]{2,1,0:T(8,128)(2,1)} %get-tuple-element.25.xs_ref, bf16[8,16,512]{2,1,0:T(8,128)(2,1)} %get-tuple-element.26.og_ref, f32[5,256]{1,0:T(8,128)} %w_in_ref.1, ...), custom_call_target="tpu_custom_call" | custom-call | tf_op jit(solution)/shard_map/closure/pallas_call | solution.py:304
  39.4 0.4 collective-permute-start.4
  39.8 1.2 %collective-permute-done.4 = f32[272,128]{1,0:T(8,128)S(1)} collective-permute-done((f32[272,128]{1,0:T(8,128)}, f32[272,128]{1,0:T(8,128)S(1)}, u32[]{:S(2)}, u32[]{:S(2)}) %collective-permute-start.4) | collective-permute-done | bytes 139296 | tf_op jit(solution)/shard_map/ppermute | solution.py:368
  41.0 0.9 add.3
  42.0 9.4 %all_to_all.26 = f32[16,17,1,128]{3,2,1,0:T(1,128)S(1)} all-to-all(f32[16,17,1,128]{3,2,1,0:T(1,128)S(1)} %bitcast.15), channel_id=1, replica_groups=mesh['zhi'=2,'y'=4,'x'=4,'zlo'=4,'core'=2] {'y','x'}, dimensions={0} | all-to-all | bytes 278528 | tf_op jit(solution)/shard_map/all_to_all | solution.py:339
  51.4 0.1 reduce_sum.28
  51.5 10.6 %all_to_all.27 = f32[8,17,1,128]{3,2,1,0:T(1,128)S(1)} all-to-all(f32[8,17,1,128]{3,2,1,0:T(1,128)S(1)} %broadcast_in_dim.7), channel_id=1, replica_groups=mesh['zhi'=2,'y'=4,'x'=4,'zlo'=4,'core'=2] {'zhi','zlo'}, dimensions={0} | all-to-all | bytes 139264 | tf_op jit(solution)/shard_map/all_to_all | solution.py:339
  62.1 0.1 reduce_sum.29
  62.2 0.1 broadcast_in_dim.8
  62.2 0.0 copy-start.8
  62.3 0.0 copy-start.7
  62.3 0.0 copy-start.10
  62.3 0.0 copy-start.9
  62.3 10.0 %all_to_all.28 = f32[16,17,1,128]{3,2,1,0:T(1,128)S(1)} all-to-all(f32[16,17,1,128]{3,2,1,0:T(1,128)S(1)} %broadcast_in_dim.8), channel_id=1, replica_groups=mesh['zhi'=2,'y'=4,'x'=4,'zlo'=4,'core'=2] {'y','x'}, dimensions={0} | all-to-all | bytes 278528 | tf_op jit(solution)/shard_map/all_to_all | solution.py:339
  72.3 0.0 copy-start
  72.3 4.4 %collective-permute-start.5 = (f32[272,128]{1,0:T(8,128)S(1)}, f32[272,128]{1,0:T(8,128)S(1)}, u32[]{:S(2)}, u32[]{:S(2)}) collective-permute-start(f32[272,128]{1,0:T(8,128)S(1)} %bitcast.13), channel_id=1, source_target_pairs={{0,1},{1,0},{2,3},{3,2},{4,5},{5,4},{6,7},{7,6},{8,9},{9,8},{10,11... | collective-permute-start | bytes 417800 | tf_op jit(solution)/shard_map/ppermute | solution.py:376
  76.7 0.0 copy-done.8
  76.7 0.3 collective-permute-start
  76.9 0.0 copy-done.7
  77.0 7.2 %collective-permute-start.1 = (f32[5,4,512]{2,1,0:T(4,128)S(1)}, f32[5,4,512]{2,1,0:T(4,128)S(1)}, u32[]{:S(2)}, u32[]{:S(2)}) collective-permute-start(f32[5,4,512]{2,1,0:T(4,128)S(1)} %copy-done.7), channel_id=1, source_target_pairs={{0,224},{32,0},{64,32},{96,64},{128,96},{160,128},{192,160},{224,1... | collective-permute-start | bytes 122888 | tf_op jit(solution)/shard_map/ppermute | solution.py:361
  84.1 0.0 copy-done.10
  84.2 5.4 %collective-permute-start.2 = (f32[5,2,512]{2,1,0:T(2,128)S(1)}, f32[5,2,512]{2,1,0:T(2,128)S(1)}, u32[]{:S(2)}, u32[]{:S(2)}) collective-permute-start(f32[5,2,512]{2,1,0:T(2,128)S(1)} %copy-done.10), channel_id=1, source_target_pairs={{0,1},{1,2},{2,3},{3,4},{4,5},{5,6},{6,7},{7,8},{8,9},{9,10},{10,1... | collective-permute-start | bytes 61448 | tf_op jit(solution)/shard_map/ppermute | solution.py:361
  89.6 0.0 copy-done.9
  89.6 0.0 collective-permute-start.3
  89.6 0.9 collective-permute-done.2.front_ref
  90.5 0.0 copy-start.5
  90.5 6.2 %collective-permute-done.3.rear_ref = f32[5,2,512]{2,1,0:T(2,128)S(1)} collective-permute-done((f32[5,2,512]{2,1,0:T(2,128)S(1)}, f32[5,2,512]{2,1,0:T(2,128)S(1)}, u32[]{:S(2)}, u32[]{:S(2)}) %collective-permute-start.3) | collective-permute-done | bytes 20512 | tf_op jit(solution)/shard_map/ppermute | solution.py:361
  96.7 0.0 copy-start.6
  96.7 0.0 collective-permute-done.left_ref
  96.7 0.0 copy-start.2
  96.7 0.0 collective-permute-done.1.right_ref
  96.7 0.0 copy-start.3
  96.7 0.0 copy-done.5
  96.7 0.6 copy-done.6
  97.3 0.0 copy-done.2
  97.3 0.0 copy-done.3
  97.3 1.8 %finish.1 = f32[5,2,4,512]{3,2,1,0:T(4,128)} custom-call(s32[2,2,4]{2,1,0:T(2,128)} %tags_ref.1, f32[5,8,512]{2,1,0:T(8,128)} %get-tuple-element.24.adj_ref, f32[4,64,128]{2,1,0:T(8,128)} %get-tuple-element.30.back_ref, f32[5,4,512]{2,1,0:T(4,128)} %copy-done.2, f32[5,4,512]{2,1,0:T(4,128)} %copy-done.3, f32[5,2,512]{2,1,0:T(2,128)} %copy-done.5, ...), custom_call_target="tpu_custom_call" | custom-call | tf_op jit(solution)/shard_map/finish/pallas_call | solution.py:325
  99.2 0.0 copy-done
  99.2 0.0 collective-permute-done.5.away_ref
  99.2 0.0 copy-start.1
  99.2 0.6 copy-done.1
  99.8 1.7 %unpack.1 = (f32[5,256]{1,0:T(8,128)}, f32[1,256]{1,0:T(1,128)}, f32[256,256]{1,0:T(8,128)}, f32[1,256]{1,0:T(1,128)}, f32[5,256]{1,0:T(8,128)}) custom-call(s32[1]{0:T(128)} %bitcast.2.core_ref, f32[272,128]{1,0:T(8,128)} %bitcast.14, f32[272,128]{1,0:T(8,128)} %copy-done.1), custom_call_target="tpu_custom_call" | custom-call | tf_op jit(solution)/shard_map/unpack/pallas_call | solution.py:261
  (3 shorter events, 0.1 us)
Async XLA Ops:
  14.4 14.5 %all-to-all-start.1 = ((f32[16,1,128]{2,1,0:T(1,128)}), f32[16,1,128]{2,1,0:T(1,128)S(1)}, u32[]{:S(2)}, u32[]{:S(2)}) async-start(f32[16,1,128]{2,1,0:T(1,128)} %broadcast_in_dim.6), calls=%async_computation.1 | async-start | bytes 16384 | tf_op jit(solution)/shard_map/all_to_all | solution.py:339
  29.0 0.6 copy-start.4
  39.4 1.6 %collective-permute-start.4 = (f32[272,128]{1,0:T(8,128)}, f32[272,128]{1,0:T(8,128)S(1)}, u32[]{:S(2)}, u32[]{:S(2)}) collective-permute-start(f32[272,128]{1,0:T(8,128)} %get-tuple-element.36), channel_id=1, source_target_pairs={{0,1},{1,0},{2,3},{3,2},{4,5},{5,4},{6,7},{7,6},{8,9},{9,8},{10,11... | collective-permute-start | bytes 417800 | tf_op jit(solution)/shard_map/ppermute | solution.py:368
  62.2 14.4 %copy-start.8 = (f32[5,4,512]{2,1,0:T(4,128)S(1)}, f32[5,4,512]{2,1,0:T(4,128)}, u32[]{:S(2)}) copy-start(f32[5,4,512]{2,1,0:T(4,128)} %get-tuple-element.31) | copy-start | bytes 122884
  62.3 14.7 %copy-start.7 = (f32[5,4,512]{2,1,0:T(4,128)S(1)}, f32[5,4,512]{2,1,0:T(4,128)}, u32[]{:S(2)}) copy-start(f32[5,4,512]{2,1,0:T(4,128)} %get-tuple-element.32) | copy-start | bytes 122884
  62.3 21.9 %copy-start.10 = (f32[5,2,512]{2,1,0:T(2,128)S(1)}, f32[5,2,512]{2,1,0:T(2,128)}, u32[]{:S(2)}) copy-start(f32[5,2,512]{2,1,0:T(2,128)} %get-tuple-element.33) | copy-start | bytes 61444
  62.3 27.3 %copy-start.9 = (f32[5,2,512]{2,1,0:T(2,128)S(1)}, f32[5,2,512]{2,1,0:T(2,128)}, u32[]{:S(2)}) copy-start(f32[5,2,512]{2,1,0:T(2,128)} %get-tuple-element.34) | copy-start | bytes 61444
  72.3 26.9 %copy-start = (f32[16,17,1,128]{3,2,1,0:T(1,128)}, f32[16,17,1,128]{3,2,1,0:T(1,128)S(1)}, u32[]{:S(2)}) copy-start(f32[16,17,1,128]{3,2,1,0:T(1,128)S(1)} %all_to_all.28) | copy-start | bytes 417796
  72.3 26.9 %collective-permute-start.5 = (f32[272,128]{1,0:T(8,128)S(1)}, f32[272,128]{1,0:T(8,128)S(1)}, u32[]{:S(2)}, u32[]{:S(2)}) collective-permute-start(f32[272,128]{1,0:T(8,128)S(1)} %bitcast.13), channel_id=1, source_target_pairs={{0,1},{1,0},{2,3},{3,2},{4,5},{5,4},{6,7},{7,6},{8,9},{9,8},{10,11... | collective-permute-start | bytes 417800 | tf_op jit(solution)/shard_map/ppermute | solution.py:376
  76.7 20.1 %collective-permute-start = (f32[5,4,512]{2,1,0:T(4,128)S(1)}, f32[5,4,512]{2,1,0:T(4,128)S(1)}, u32[]{:S(2)}, u32[]{:S(2)}) collective-permute-start(f32[5,4,512]{2,1,0:T(4,128)S(1)} %copy-done.8), channel_id=1, source_target_pairs={{0,32},{32,64},{64,96},{96,128},{128,160},{160,192},{192,224},{224... | collective-permute-start | bytes 122888 | tf_op jit(solution)/shard_map/ppermute | solution.py:361
  77.0 19.8 %collective-permute-start.1 = (f32[5,4,512]{2,1,0:T(4,128)S(1)}, f32[5,4,512]{2,1,0:T(4,128)S(1)}, u32[]{:S(2)}, u32[]{:S(2)}) collective-permute-start(f32[5,4,512]{2,1,0:T(4,128)S(1)} %copy-done.7), channel_id=1, source_target_pairs={{0,224},{32,0},{64,32},{96,64},{128,96},{160,128},{192,160},{224,1... | collective-permute-start | bytes 122888 | tf_op jit(solution)/shard_map/ppermute | solution.py:361
  84.2 6.4 %collective-permute-start.2 = (f32[5,2,512]{2,1,0:T(2,128)S(1)}, f32[5,2,512]{2,1,0:T(2,128)S(1)}, u32[]{:S(2)}, u32[]{:S(2)}) collective-permute-start(f32[5,2,512]{2,1,0:T(2,128)S(1)} %copy-done.10), channel_id=1, source_target_pairs={{0,1},{1,2},{2,3},{3,4},{4,5},{5,6},{6,7},{7,8},{8,9},{9,10},{10,1... | collective-permute-start | bytes 61448 | tf_op jit(solution)/shard_map/ppermute | solution.py:361
  89.6 7.1 %collective-permute-start.3 = (f32[5,2,512]{2,1,0:T(2,128)S(1)}, f32[5,2,512]{2,1,0:T(2,128)S(1)}, u32[]{:S(2)}, u32[]{:S(2)}) collective-permute-start(f32[5,2,512]{2,1,0:T(2,128)S(1)} %copy-done.9), channel_id=1, source_target_pairs={{0,31},{1,0},{2,1},{3,2},{4,3},{5,4},{6,5},{7,6},{8,7},{9,8},{10,9... | collective-permute-start | bytes 61448 | tf_op jit(solution)/shard_map/ppermute | solution.py:361
  90.5 6.2 %copy-start.5 = (f32[5,2,512]{2,1,0:T(2,128)}, f32[5,2,512]{2,1,0:T(2,128)S(1)}, u32[]{:S(2)}) copy-start(f32[5,2,512]{2,1,0:T(2,128)S(1)} %collective-permute-done.2.front_ref) | copy-start | bytes 61444
  96.7 0.6 copy-start.6
  96.7 0.6 copy-start.2
  96.7 0.6 copy-start.3
  99.2 0.7 copy-start.1

commit v5 on v4

--- a/solution.py
+++ b/solution.py
@@ -16,8 +16,7 @@
 AXES = ("zhi", "y", "x", "zlo", "core")
 GX = ("zhi", "y")
 GZ = ("x", "zlo", "core")
-PLANE = ("y", "x")
-COLUMN = ("zhi", "zlo", "core")
+PLANE = ("y", "x", "core")
 TOWER = ("zhi", "zlo")
 LANES = 128
 NODES = 64
@@ -119,9 +118,9 @@
 
 def closure_kernel(
     entries,
-    core_ref, squares_ref, xs_ref, og_ref, w_in_ref, b_in_ref, w_mid_ref, w_mid_t_ref, b_col_ref, w_out_ref,
-    back_ref, mine_ref, other_ref,
-    mid_ref, in_ref, out_ref, wide_ref,
+    squares_ref, xs_ref, og_ref, w_in_ref, b_in_ref, w_mid_ref, w_mid_t_ref, b_col_ref, w_out_ref,
+    back_ref, sums_ref,
+    mid_ref, in_ref, out_ref,
 ):
     cells = xs_ref.shape[0]
     channels, hidden = w_in_ref.shape
@@ -177,15 +176,10 @@
         ],
         axis=0,
     )
-    half = hidden // 2
-    wide_ref[0] = extra[:, :half]
-    wide_ref[1] = extra[:, half:]
-    core = core_ref[0]
-    for ref, place in ((mine_ref, core), (other_ref, 1 - core)):
-        start = pl.multiple_of(place * half, half)
-        ref[:half, :] = mid_ref[pl.ds(start, half), :half]
-        ref[half:hidden, :] = mid_ref[pl.ds(start, half), half:]
-        ref[hidden:, :] = wide_ref[place]
+    sums_ref[:hidden, :] = mid_ref[:hidden, :LANES]
+    sums_ref[hidden : 2 * hidden, :] = mid_ref[:hidden, LANES:]
+    sums_ref[2 * hidden : 2 * hidden + 2 * GROUP, :] = extra[:, :LANES]
+    sums_ref[2 * hidden + 2 * GROUP :, :] = extra[:, LANES:]
 
 
 def finish_kernel(
@@ -226,16 +220,13 @@
         out_ref[c, 1] = total[span:]
 
 
-def unpack_kernel(core_ref, own_ref, away_ref, in_ref, b_in_ref, mid_ref, b_mid_ref, out_ref):
+def unpack_kernel(sums_ref, in_ref, b_in_ref, mid_ref, b_mid_ref, out_ref):
     channels, hidden = in_ref.shape
-    half = hidden // 2
-    own, away = own_ref[...], away_ref[...]
-    first = jnp.where(core_ref[0] == 0, own, away)
-    second = jnp.where(core_ref[0] == 0, away, own)
-    for k, part in enumerate((first, second)):
-        mid_ref[k * half : (k + 1) * half, :half] = part[:half]
-        mid_ref[k * half : (k + 1) * half, half:] = part[half:hidden]
-    extra = jnp.concatenate([first[hidden:], second[hidden:]], axis=1)
+    mid_ref[:, :LANES] = sums_ref[:hidden, :]
+    mid_ref[:, LANES:] = sums_ref[hidden : 2 * hidden, :]
+    extra = jnp.concatenate(
+        [sums_ref[2 * hidden : 2 * hidden + 2 * GROUP, :], sums_ref[2 * hidden + 2 * GROUP :, :]], axis=1
+    )
     in_ref[...] = extra[:channels]
     b_in_ref[...] = extra[channels : channels + 1]
     out_ref[...] = extra[GROUP : GROUP + channels]
@@ -256,8 +247,8 @@
     )(state)
 
 
-def run_unpack(core, own, away, channels):
-    hidden = own.shape[0] - 2 * GROUP
+def run_unpack(sums, channels):
+    hidden = (sums.shape[0] - 4 * GROUP) // 2
     return pl.pallas_call(
         unpack_kernel,
         out_shape=(
@@ -267,10 +258,10 @@
             shape(1, hidden),
             shape(channels, hidden),
         ),
-        in_specs=[pl.BlockSpec(memory_space=pltpu.SMEM)] + whole_vmem(2),
+        in_specs=whole_vmem(1),
         out_specs=tuple(whole_vmem(5)),
         name="unpack",
-    )(core, own, away)
+    )(sums)
 
 
 def run_adjoint(state, cotangent, local_inverse, w_mid, b_mid, w_out):
@@ -298,26 +289,24 @@
     )(state, cotangent, local_inverse, w_mid, b_mid.reshape(1, hidden), w_out.T)
 
 
-def run_closure(entries, core, squares, xs, og, w_in, b_in, w_mid, w_mid_t, b_col, w_out):
+def run_closure(entries, squares, xs, og, w_in, b_in, w_mid, w_mid_t, b_col, w_out):
     cells, _, line = xs.shape
     _, hidden = w_in.shape
     return pl.pallas_call(
         functools.partial(closure_kernel, entries),
         out_shape=(
             shape(line // LANES, cells * GROUP, LANES),
-            shape(hidden + 2 * GROUP, LANES),
-            shape(hidden + 2 * GROUP, LANES),
+            shape(2 * hidden + 4 * GROUP, LANES),
         ),
-        in_specs=[pl.BlockSpec(memory_space=pltpu.SMEM)] + whole_vmem(9),
-        out_specs=tuple(whole_vmem(3)),
+        in_specs=whole_vmem(9),
+        out_specs=tuple(whole_vmem(2)),
         scratch_shapes=[
             pltpu.VMEM((hidden + 2 * GROUP, hidden), F32),
             pltpu.VMEM((2 * GROUP, hidden), F32),
             pltpu.VMEM((2 * GROUP, hidden), F32),
-            pltpu.VMEM((2, 2 * GROUP, LANES), F32),
         ],
         name="closure",
-    )(core, squares, xs, og, w_in, b_in.reshape(1, hidden), w_mid, w_mid_t, b_col, w_out)
+    )(squares, xs, og, w_in, b_in.reshape(1, hidden), w_mid, w_mid_t, b_col, w_out)
 
 
 def run_finish(tags, adjoint, back, left, right, front, rear):
@@ -344,14 +333,9 @@
     gx, gz = lax.axis_size(GX), lax.axis_size(GZ)
     devices = gx * gz
     nodes = x_elems * z_elems * line * devices
-    swap = [(0, 1), (1, 0)]
-    core = lax.axis_index("core")
-
-    plane, column, tower = lax.axis_size(PLANE), lax.axis_size(COLUMN), lax.axis_size(TOWER)
-    squares = run_squares(state, plane).reshape(plane, 1, LANES)
-    squares = exchange(squares, PLANE)
-    squares = jnp.broadcast_to(jnp.sum(squares, axis=0, keepdims=True), (column, 1, LANES))
-    squares = exchange(squares, COLUMN)
+    plane, tower = lax.axis_size(PLANE), lax.axis_size(TOWER)
+    squares = run_squares(state, devices).reshape(devices, 1, LANES)
+    squares = exchange(squares, AXES)
     adjoint, og, xs, w_mid_t, b_col, w_wide, low_x, high_x, low_z, high_z = run_adjoint(
         state, cotangent, local_inverse, w_mid, b_mid, w_out
     )
@@ -359,22 +343,20 @@
     halo = []
     for face, axes, count, way in sends:
         halo.append(lax.ppermute(face, axes, ring(count, way)))
-    core = core.reshape(1)
-    back, mine, other = run_closure(
-        float(channels * nodes), core, squares.reshape(column, LANES), xs, og, w_in, b_in, w_mid,
+    back, sums = run_closure(
+        float(channels * nodes), squares.reshape(devices, LANES), xs, og, w_in, b_in, w_mid,
         w_mid_t, b_col, w_wide,
     )
     grad_state = run_finish(wall_tags, adjoint, back, *halo)
-    mine = mine + lax.ppermute(other, "core", swap)
     factor = 4.0 / math.sqrt(nodes)
-    width = mine.shape[0] // plane
-    part = exchange(mine.reshape(plane, width, 1, LANES), PLANE)
+    width = sums.shape[0] // plane
+    part = exchange(sums.reshape(plane, width, 1, LANES), PLANE)
     part = jnp.broadcast_to(jnp.sum(part, axis=0, keepdims=True), (tower, width, 1, LANES))
     part = exchange(part, TOWER)
-    part = jnp.broadcast_to(factor * jnp.sum(part, axis=0, keepdims=True), (plane, width, 1, LANES))
-    own = exchange(part, PLANE).reshape(mine.shape)
-    away = lax.ppermute(own, "core", swap)
-    grad_in, grad_b_in, grad_mid, grad_b_mid, grad_out = run_unpack(core, own, away, channels)
+    part = factor * jnp.sum(part, axis=0, keepdims=True)
+    part = jnp.broadcast_to(part, (plane, width, 1, LANES))
+    part = exchange(part, PLANE)
+    grad_in, grad_b_in, grad_mid, grad_b_mid, grad_out = run_unpack(part.reshape(sums.shape), channels)
     return grad_state, grad_in, grad_b_in[0], grad_mid, grad_b_mid[0], grad_out.T
 
 

time: 102 us -> 90 us (0.88)
  the two profiles are of different devices: /device:TPU:103 before, /device:TPU:97 now
where the time goes in v5:
time: 90 us; the launch traced here: 89.5 us
  starting transfers between devices  32.2 us (36%)
  blocking collectives  22.5 us (25%)
  Pallas kernels  20.3 us (23%)
  waiting for transfers between devices  10.7 us (12%)
  local copies, waits for them, and re-layouts  2.86 us (3%)
    all_to_all x2, blocking collectives, exchange(): return lax.all_to_all(value, axes, 0, 0, tiled=True)  22.5 us
    all_to_all x2, starting transfers between devices, exchange(): return lax.all_to_all(value, axes, 0, 0, tiled=True)  19.6 us
    ppermute x4, starting transfers between devices, per_device(): halo.append(lax.ppermute(face, axes, ring(count, way)))  12.6 us
    pallas_call x1, Pallas kernels, run_closure(): pl.pallas_call(functools.partial(closure_kernel, entries), out_shape=(sha...  9.93 us
    ppermute x4, waiting for transfers between devices, per_device(): halo.append(lax.ppermute(face, axes, ring(count, way)))  5.9 us
    pallas_call x1, Pallas kernels, run_adjoint(): pl.pallas_call(adjoint_kernel, out_shape=(shape(channels, cells, line), s...  5.15 us
    all_to_all x2, waiting for transfers between devices, exchange(): return lax.all_to_all(value, axes, 0, 0, tiled=True)  4.78 us
    unnamed x20, local copies, waits for them, and re-layouts  1.98 us
  transfers between devices with their start and end apart: 6, of which 3 were waited for; matrix products, arithmetic and copies ran while one was open for 0% of the time, Pallas kernels for 8%

profile of v5, /device:TPU:97, one launch (start us, length us, event | category | flops | bytes accessed | tf_op | source)
XLA Modules:
  0.0 89.5 jit_solution(6654796322764455311)
XLA Ops:
  0.6 1.7 %squares.1 = f32[256,128]{1,0:T(8,128)} custom-call(f32[5,2,4,512]{3,2,1,0:T(4,128)} %state_ref.3), custom_call_target="tpu_custom_call" | custom-call | tf_op jit(solution)/shard_map/squares/pallas_call | solution.py:241
  2.3 14.3 %all-to-all-start = ((f32[256,1,128]{2,1,0:T(1,128)}), f32[256,1,128]{2,1,0:T(1,128)S(1)}, u32[]{:S(2)}, u32[]{:S(2)}) async-start(f32[256,1,128]{2,1,0:T(1,128)} %bitcast.14), calls=%async_computation | async-start | bytes 262144 | tf_op jit(solution)/shard_map/all_to_all | solution.py:328
  16.6 5.2 %adjoint.1 = (f32[5,8,512]{2,1,0:T(8,128)}, bf16[8,16,512]{2,1,0:T(8,128)(2,1)}, bf16[8,32,512]{2,1,0:T(8,128)(2,1)}, bf16[256,256]{1,0:T(8,128)(2,1)}, f32[256,...) custom-call(f32[5,2,4,512]{3,2,1,0:T(4,128)} %state_ref.3, ...), custom_call_target="tpu_custom_call" | custom-call | tf_op jit(solution)/shard_map/adjoint/pallas_call | solution.py:271
  21.8 4.8 %all-to-all-done = f32[256,1,128]{2,1,0:T(1,128)S(1)} async-done(((f32[256,1,128]{2,1,0:T(1,128)}), f32[256,1,128]{2,1,0:T(1,128)S(1)}, u32[]{:S(2)}, u32[]{:S(2)}) %all-to-all-start) | async-done | bytes 131104 | tf_op jit(solution)/shard_map/all_to_all | solution.py:328
  26.6 0.0 copy-start.1
  26.6 0.6 copy-done.1
  27.2 9.9 %closure.1 = (f32[4,64,128]{2,1,0:T(8,128)}, f32[544,128]{1,0:T(8,128)}) custom-call(f32[256,128]{1,0:T(8,128)} %bitcast.13, bf16[8,32,512]{2,1,0:T(8,128)(2,1)} %get-tuple-element.24.xs_ref, bf16[8,16,512]{2,1,0:T(8,128)(2,1)} %get-tuple-element.25.og_ref, f32[5,256]{1,0:T(8,128)} %w_in_ref.1, f32[1,256]{1,0:T(1,128)} %bitcast.18, ...), custom_call_target="tpu_custom_call" | custom-call | tf_op jit(solution)/shard_map/closure/pallas_call | solution.py:295
  37.1 13.3 %all_to_all.20 = f32[32,17,1,128]{3,2,1,0:T(1,128)S(1)} all-to-all(f32[32,17,1,128]{3,2,1,0:T(1,128)} %bitcast.15), channel_id=1, replica_groups=mesh['zhi'=2,'y'=4,'x'=4,'zlo'=4,'core'=2] {'y','x','core'}, dimensions={0} | all-to-all | bytes 557056 | tf_op jit(solution)/shard_map/all_to_all | solution.py:328
  50.4 0.2 reduce_sum.18
  50.6 9.3 %all_to_all.21 = f32[8,17,1,128]{3,2,1,0:T(1,128)S(1)} all-to-all(f32[8,17,1,128]{3,2,1,0:T(1,128)S(1)} %broadcast_in_dim.4), channel_id=1, replica_groups=mesh['zhi'=2,'y'=4,'x'=4,'zlo'=4,'core'=2] {'zhi','zlo'}, dimensions={0} | all-to-all | bytes 139264 | tf_op jit(solution)/shard_map/all_to_all | solution.py:328
  59.9 0.1 reduce_sum.19
  60.0 0.8 broadcast_in_dim.5
  60.8 0.0 copy-start.7
  60.8 0.0 copy-start.6
  60.8 0.0 copy-start.9
  60.8 0.0 copy-start.8
  60.8 5.3 %all-to-all-start.3 = ((f32[32,17,1,128]{3,2,1,0:T(1,128)}), f32[32,17,1,128]{3,2,1,0:T(1,128)S(1)}, u32[]{:S(2)}, u32[]{:S(2)}) async-start(f32[32,17,1,128]{3,2,1,0:T(1,128)} %broadcast_in_dim.5), calls=%async_computation.3 | async-start | bytes 557056 | tf_op jit(solution)/shard_map/all_to_all | solution.py:328
  66.1 0.0 copy-done.7
  66.1 1.5 %collective-permute-start = (f32[5,4,512]{2,1,0:T(4,128)S(1)}, f32[5,4,512]{2,1,0:T(4,128)S(1)}, u32[]{:S(2)}, u32[]{:S(2)}) collective-permute-start(f32[5,4,512]{2,1,0:T(4,128)S(1)} %copy-done.7), channel_id=1, source_target_pairs={{0,32},{32,64},{64,96},{96,128},{128,160},{160,192},{192,224},{224... | collective-permute-start | bytes 122888 | tf_op jit(solution)/shard_map/ppermute | solution.py:345
  67.6 0.0 copy-done.6
  67.6 6.1 %collective-permute-start.1 = (f32[5,4,512]{2,1,0:T(4,128)S(1)}, f32[5,4,512]{2,1,0:T(4,128)S(1)}, u32[]{:S(2)}, u32[]{:S(2)}) collective-permute-start(f32[5,4,512]{2,1,0:T(4,128)S(1)} %copy-done.6), channel_id=1, source_target_pairs={{0,224},{32,0},{64,32},{96,64},{128,96},{160,128},{192,160},{224,1... | collective-permute-start | bytes 122888 | tf_op jit(solution)/shard_map/ppermute | solution.py:345
  73.7 0.0 copy-done.9
  73.7 5.0 %collective-permute-start.2 = (f32[5,2,512]{2,1,0:T(2,128)S(1)}, f32[5,2,512]{2,1,0:T(2,128)S(1)}, u32[]{:S(2)}, u32[]{:S(2)}) collective-permute-start(f32[5,2,512]{2,1,0:T(2,128)S(1)} %copy-done.9), channel_id=1, source_target_pairs={{0,1},{1,2},{2,3},{3,4},{4,5},{5,6},{6,7},{7,8},{8,9},{9,10},{10,1... | collective-permute-start | bytes 61448 | tf_op jit(solution)/shard_map/ppermute | solution.py:345
  78.7 0.0 copy-done.8
  78.7 0.0 collective-permute-start.3
  78.7 0.9 %collective-permute-done.2.front_ref = f32[5,2,512]{2,1,0:T(2,128)S(1)} collective-permute-done((f32[5,2,512]{2,1,0:T(2,128)S(1)}, f32[5,2,512]{2,1,0:T(2,128)S(1)}, u32[]{:S(2)}, u32[]{:S(2)}) %collective-permute-start.2) | collective-permute-done | bytes 20512 | tf_op jit(solution)/shard_map/ppermute | solution.py:345
  79.6 0.0 copy-start.4
  79.6 5.0 %collective-permute-done.3.rear_ref = f32[5,2,512]{2,1,0:T(2,128)S(1)} collective-permute-done((f32[5,2,512]{2,1,0:T(2,128)S(1)}, f32[5,2,512]{2,1,0:T(2,128)S(1)}, u32[]{:S(2)}, u32[]{:S(2)}) %collective-permute-start.3) | collective-permute-done | bytes 20512 | tf_op jit(solution)/shard_map/ppermute | solution.py:345
  84.6 0.0 copy-start.5
  84.6 0.0 collective-permute-done.left_ref
  84.6 0.0 copy-start.2
  84.6 0.0 collective-permute-done.1.right_ref
  84.6 0.0 copy-start.3
  84.6 0.0 copy-done.4
  84.6 0.6 copy-done.5
  85.2 0.0 copy-done.2
  85.2 0.0 copy-done.3
  85.2 1.8 %finish.1 = f32[5,2,4,512]{3,2,1,0:T(4,128)} custom-call(s32[2,2,4]{2,1,0:T(2,128)} %tags_ref.1, f32[5,8,512]{2,1,0:T(8,128)} %get-tuple-element.23.adj_ref, f32[4,64,128]{2,1,0:T(8,128)} %get-tuple-element.29.back_ref, f32[5,4,512]{2,1,0:T(4,128)} %copy-done.2, f32[5,4,512]{2,1,0:T(4,128)} %copy-done.3, f32[5,2,512]{2,1,0:T(2,128)} %copy-done.4, ...), custom_call_target="tpu_custom_call" | custom-call | tf_op jit(solution)/shard_map/finish/pallas_call | solution.py:314
  87.1 0.0 all-to-all-done.3
  87.1 0.0 copy-start
  87.1 0.7 copy-done
  87.8 1.7 %unpack.1 = (f32[5,256]{1,0:T(8,128)}, f32[1,256]{1,0:T(1,128)}, f32[256,256]{1,0:T(8,128)}, f32[1,256]{1,0:T(1,128)}, f32[5,256]{1,0:T(8,128)}) custom-call(f32[544,128]{1,0:T(8,128)} %bitcast.12), custom_call_target="tpu_custom_call" | custom-call | tf_op jit(solution)/shard_map/unpack/pallas_call | solution.py:252
  (2 shorter events, 0.0 us)
Async XLA Ops:
  2.3 24.2 %all-to-all-start = ((f32[256,1,128]{2,1,0:T(1,128)}), f32[256,1,128]{2,1,0:T(1,128)S(1)}, u32[]{:S(2)}, u32[]{:S(2)}) async-start(f32[256,1,128]{2,1,0:T(1,128)} %bitcast.14), calls=%async_computation | async-start | bytes 262144 | tf_op jit(solution)/shard_map/all_to_all | solution.py:328
  26.6 0.7 copy-start.1
  60.8 5.3 %copy-start.7 = (f32[5,4,512]{2,1,0:T(4,128)S(1)}, f32[5,4,512]{2,1,0:T(4,128)}, u32[]{:S(2)}) copy-start(f32[5,4,512]{2,1,0:T(4,128)} %get-tuple-element.30) | copy-start | bytes 122884
  60.8 6.8 %copy-start.6 = (f32[5,4,512]{2,1,0:T(4,128)S(1)}, f32[5,4,512]{2,1,0:T(4,128)}, u32[]{:S(2)}) copy-start(f32[5,4,512]{2,1,0:T(4,128)} %get-tuple-element.31) | copy-start | bytes 122884
  60.8 12.8 %copy-start.9 = (f32[5,2,512]{2,1,0:T(2,128)S(1)}, f32[5,2,512]{2,1,0:T(2,128)}, u32[]{:S(2)}) copy-start(f32[5,2,512]{2,1,0:T(2,128)} %get-tuple-element.32) | copy-start | bytes 61444
  60.8 17.9 %copy-start.8 = (f32[5,2,512]{2,1,0:T(2,128)S(1)}, f32[5,2,512]{2,1,0:T(2,128)}, u32[]{:S(2)}) copy-start(f32[5,2,512]{2,1,0:T(2,128)} %get-tuple-element.33) | copy-start | bytes 61444
  60.8 26.3 %all-to-all-start.3 = ((f32[32,17,1,128]{3,2,1,0:T(1,128)}), f32[32,17,1,128]{3,2,1,0:T(1,128)S(1)}, u32[]{:S(2)}, u32[]{:S(2)}) async-start(f32[32,17,1,128]{3,2,1,0:T(1,128)} %broadcast_in_dim.5), calls=%async_computation.3 | async-start | bytes 557056 | tf_op jit(solution)/shard_map/all_to_all | solution.py:328
  66.1 18.5 %collective-permute-start = (f32[5,4,512]{2,1,0:T(4,128)S(1)}, f32[5,4,512]{2,1,0:T(4,128)S(1)}, u32[]{:S(2)}, u32[]{:S(2)}) collective-permute-start(f32[5,4,512]{2,1,0:T(4,128)S(1)} %copy-done.7), channel_id=1, source_target_pairs={{0,32},{32,64},{64,96},{96,128},{128,160},{160,192},{192,224},{224... | collective-permute-start | bytes 122888 | tf_op jit(solution)/shard_map/ppermute | solution.py:345
  67.6 17.0 %collective-permute-start.1 = (f32[5,4,512]{2,1,0:T(4,128)S(1)}, f32[5,4,512]{2,1,0:T(4,128)S(1)}, u32[]{:S(2)}, u32[]{:S(2)}) collective-permute-start(f32[5,4,512]{2,1,0:T(4,128)S(1)} %copy-done.6), channel_id=1, source_target_pairs={{0,224},{32,0},{64,32},{96,64},{128,96},{160,128},{192,160},{224,1... | collective-permute-start | bytes 122888 | tf_op jit(solution)/shard_map/ppermute | solution.py:345
  73.7 5.9 %collective-permute-start.2 = (f32[5,2,512]{2,1,0:T(2,128)S(1)}, f32[5,2,512]{2,1,0:T(2,128)S(1)}, u32[]{:S(2)}, u32[]{:S(2)}) collective-permute-start(f32[5,2,512]{2,1,0:T(2,128)S(1)} %copy-done.9), channel_id=1, source_target_pairs={{0,1},{1,2},{2,3},{3,4},{4,5},{5,6},{6,7},{7,8},{8,9},{9,10},{10,1... | collective-permute-start | bytes 61448 | tf_op jit(solution)/shard_map/ppermute | solution.py:345
  78.7 5.9 %collective-permute-start.3 = (f32[5,2,512]{2,1,0:T(2,128)S(1)}, f32[5,2,512]{2,1,0:T(2,128)S(1)}, u32[]{:S(2)}, u32[]{:S(2)}) collective-permute-start(f32[5,2,512]{2,1,0:T(2,128)S(1)} %copy-done.8), channel_id=1, source_target_pairs={{0,31},{1,0},{2,1},{3,2},{4,3},{5,4},{6,5},{7,6},{8,7},{9,8},{10,9... | collective-permute-start | bytes 61448 | tf_op jit(solution)/shard_map/ppermute | solution.py:345
  79.6 5.0 %copy-start.4 = (f32[5,2,512]{2,1,0:T(2,128)}, f32[5,2,512]{2,1,0:T(2,128)S(1)}, u32[]{:S(2)}) copy-start(f32[5,2,512]{2,1,0:T(2,128)S(1)} %collective-permute-done.2.front_ref) | copy-start | bytes 61444
  84.6 0.6 copy-start.5
  84.6 0.6 copy-start.2
  84.6 0.6 copy-start.3
  87.1 0.7 copy-start
